TPU v7x, 1024 devices: a whole 4x4x32 slice. The times are simulated.
1024 devices in a mesh: tok: 128 (over y, z), head: 8 (over x, core).
Axes of the slice: x: 4, y: 4, z: 32, core: 2. Of those that a mesh axis runs over, the one named last changes fastest.
Arguments:
- query: bfloat16 [16384, 8192], P('tok', 'head'), may hold values from -5 to 5
- keys: bfloat16 [16384, 1024], P(('tok', 'head')), may hold values from -5 to 5
- values: bfloat16 [16384, 1024], P(('tok', 'head')), may hold values from -6 to 6
- out_grad: bfloat16 [16384, 8192], P('tok', 'head'), may hold values from -6 to 6
- log_norm: float32 [64, 16384], P('head', 'tok'), may hold values from 4 to 6
- row_dot: float32 [64, 16384], P('head', 'tok'), may hold values from -24 to 24
- doc_start: int32 [16384], replicated, may hold values from 0 to 16383, as said below
- spans: int32 [128], replicated, may hold values from 1 to 6, as said below
Outputs:
- query_grad: bfloat16 [16384, 8192], P('tok', 'head')
- key_grad: bfloat16 [16384, 1024], P('tok', 'head')
- value_grad: bfloat16 [16384, 1024], P('tok', 'head')
Inputs may be any that keep to these rules, and one draw needn't show every extreme that they name: doc_start[t] <= t, doc_start[0] = 0, doc_start never falls along t, and doc_start[t] = t where a document begins; the last position always begins a document of one token. Query block g (tokens g * 128 to g * 128 + 127) reads the spans[g] key blocks that end with block g itself. In every draw at least one query block has span 6.
All inputs are finite; a program needn't handle non-finite values.
Results may differ from a plain program's by a relative error of at most 0.008.
Values may be sent and summed in bfloat16 or wider, within the bound.
A program may use at most 32 MiB of HBM per device.

v0:
```python
import math

import jax
import jax.numpy as jnp
from jax import lax
from jax.sharding import PartitionSpec as P

HEADS = 64
KV_HEADS = 8
HEAD_DIM = 128
QBLOCK = 128
REACH = 5


def from_behind(value, axis, steps):
    count = lax.axis_size(axis)
    initial, last = (max(0, -steps), min(count, count - steps))
    return lax.ppermute(value, axis, [(source, source + steps) for source in range(initial, last)])


def block_grads(
    query_block, outgrad_block, key_block, value_block, norm_block, dot_block, allowed, head_scale
):
    scores = (
        jnp.einsum("qagd,kad->agqk", query_block, key_block, preferred_element_type=jnp.float32)
        * head_scale
    )
    probs = jnp.where(allowed[None, None], jnp.exp(scores - norm_block[..., None]), 0.0)
    probs_low = probs.astype(jnp.bfloat16)
    value_term = jnp.einsum(
        "agqk,qagd->kad", probs_low, outgrad_block, preferred_element_type=jnp.float32
    )
    prob_grad = jnp.einsum(
        "qagd,kad->agqk", outgrad_block, value_block, preferred_element_type=jnp.float32
    )
    score_grad = (probs * (prob_grad - dot_block[..., None])).astype(jnp.bfloat16)
    query_term = (
        jnp.einsum("agqk,kad->qagd", score_grad, key_block, preferred_element_type=jnp.float32)
        * head_scale
    )
    key_term = (
        jnp.einsum("agqk,qagd->kad", score_grad, query_block, preferred_element_type=jnp.float32)
        * head_scale
    )
    return (query_term, key_term, value_term)


def run_items(
    query_all,
    outgrad_all,
    norm_all,
    dot_all,
    window_all,
    start_all,
    span_all,
    base_all,
    first_item,
    last_item,
    reach_back,
    head_scale,
):
    sources, blocks_here = span_all.shape
    flat_spans = span_all.reshape(-1)
    span_ends = jnp.cumsum(flat_spans)
    row_index = jnp.arange(QBLOCK, dtype=jnp.int32)
    key_cols = window_all.shape[-1]
    heads_kv = query_all.shape[3]
    zero_index = jnp.int32(0)

    def one_item(item_index, totals):
        query_acc, pair_acc = totals
        flat_index = jnp.sum((span_ends <= item_index).astype(jnp.int32))
        offset = item_index - (span_ends[flat_index] - flat_spans[flat_index])
        source = flat_index // blocks_here
        block_index = flat_index % blocks_here
        key_index = reach_back * blocks_here + block_index - offset
        query_block = query_all[source, block_index]
        outgrad_block = outgrad_all[source, block_index]
        norm_block = norm_all[source, block_index]
        dot_block = dot_all[source, block_index]
        corner = (source, zero_index, key_index * QBLOCK, zero_index)
        key_pair = lax.dynamic_slice(window_all, corner, (1, 2, QBLOCK, key_cols))[0]
        key_pair = key_pair.reshape(2, QBLOCK, heads_kv, key_cols // heads_kv)
        starts = start_all[0]
        query_pos = (base_all[source] + block_index) * QBLOCK + row_index
        key_pos = (base_all[source] + block_index - offset) * QBLOCK + row_index
        allowed = (key_pos[None, :] <= query_pos[:, None]) & (key_pos[None, :] >= starts[:, None])
        query_term, key_term, value_term = block_grads(
            query_block,
            outgrad_block,
            key_pair[0],
            key_pair[1],
            norm_block,
            dot_block,
            allowed,
            head_scale,
        )
        query_acc = query_acc.at[source, block_index].add(query_term)
        fresh_terms = jnp.stack([key_term, value_term]).reshape(1, 2, QBLOCK, key_cols)
        current = lax.dynamic_slice(pair_acc, corner, fresh_terms.shape)
        pair_acc = lax.dynamic_update_slice(pair_acc, current + fresh_terms, corner)
        return (query_acc, pair_acc)

    query_zero = jnp.zeros(query_all.shape, jnp.float32)
    pair_zero = jnp.zeros(window_all.shape, jnp.float32)
    return lax.fori_loop(first_item, last_item, one_item, (query_zero, pair_zero))


def per_device(query, keys, values, out_grad, log_norm, row_dot, doc_start, spans):
    head_scale = 1.0 / math.sqrt(HEAD_DIM)
    tok_rows = query.shape[0]
    blocks_here = tok_rows // QBLOCK
    kv_local = KV_HEADS // lax.axis_size("head")
    group_size = HEADS // KV_HEADS
    reach_back = REACH
    key_pair = lax.all_to_all(
        jnp.stack([keys, values]), "head", split_axis=2, concat_axis=1, tiled=True
    )
    pieces = []
    for steps_back in range(reach_back, 0, -1):
        keep_rows = tok_rows
        arrived = from_behind(key_pair, "tok", steps_back)
        pieces.append(arrived)
    pieces.append(key_pair)
    window = jnp.concatenate(pieces, axis=1)
    query_blocks = query.reshape(blocks_here, QBLOCK, kv_local, group_size, HEAD_DIM)
    outgrad_blocks = out_grad.reshape(blocks_here, QBLOCK, kv_local, group_size, HEAD_DIM)
    norm_blocks = log_norm.reshape(kv_local, group_size, blocks_here, QBLOCK).transpose(2, 0, 1, 3)
    dot_blocks = row_dot.reshape(kv_local, group_size, blocks_here, QBLOCK).transpose(2, 0, 1, 3)
    tok_index = lax.axis_index("tok")
    my_base = tok_index * blocks_here
    my_starts = lax.dynamic_slice_in_dim(doc_start, my_base * QBLOCK, tok_rows)
    my_spans = lax.dynamic_slice_in_dim(spans, my_base, blocks_here)
    query_acc, pair_acc = run_items(
        query_blocks[None],
        outgrad_blocks[None],
        norm_blocks[None],
        dot_blocks[None],
        window[None],
        my_starts[None],
        my_spans[None],
        my_base[None],
        jnp.int32(0),
        jnp.sum(my_spans),
        reach_back,
        head_scale,
    )
    query_sum = query_acc[0]
    pair_sum = pair_acc[0]
    own_pair = pair_sum[:, reach_back * tok_rows :]
    for steps_back in range(1, reach_back + 1):
        keep_rows = tok_rows
        segment_end = (reach_back - steps_back + 1) * tok_rows
        segment = pair_sum[:, segment_end - keep_rows : segment_end]
        arrived = from_behind(segment, "tok", -steps_back)
        own_pair = own_pair.at[:, tok_rows - keep_rows :].add(arrived)
    query_grad = query_sum.reshape(tok_rows, kv_local * group_size * HEAD_DIM).astype(jnp.bfloat16)
    key_grad = own_pair[0].astype(jnp.bfloat16)
    value_grad = own_pair[1].astype(jnp.bfloat16)
    return (query_grad, key_grad, value_grad)


def solution(mesh):
    in_specs = (
        P("tok", "head"),
        P(("tok", "head"), None),
        P(("tok", "head"), None),
        P("tok", "head"),
        P("head", "tok"),
        P("head", "tok"),
        P(),
        P(),
    )
    out_specs = (P("tok", "head"), P("tok", "head"), P("tok", "head"))
    return jax.shard_map(
        per_device, mesh=mesh, in_specs=in_specs, out_specs=out_specs, check_vma=False
    )
```

profile of v0, /device:TPU:24, one launch (start us, length us, event | category | flops | bytes accessed | tf_op | source)
XLA Modules:
  0.0 121.0 jit_solution(460859237055444034)
XLA Ops:
  0.6 0.8 pad_maximum_fusion
  2.3 9.7 %all_to_all.18 = bf16[8,2,2048]{2,1,0:T(2,128)(2,1)S(1)} all-to-all(bf16[8,2,2048]{2,1,0:T(2,128)(2,1)S(1)} %reshape.480), channel_id=1, replica_groups=mesh['tok'=128,'head'=8] {'head'}, dimensions={0} | all-to-all | bytes 131072 | tf_op jit(solution)/shard_map/all_to_all | solution.py:116
  12.8 10.5 %collective-permute-start = (bf16[2,128,128]{2,1,0:T(8,128)(2,1)S(1)}, bf16[2,128,128]{2,1,0:T(8,128)(2,1)S(1)}, u32[]{:S(2)}, u32[]{:S(2)}) collective-permute-start(bf16[2,128,128]{2,1,0:T(8,128)(2,1)S(1)} %bitcast.174), channel_id=1, source_target_pairs={{0,40},{8,48},{16,56},{24,64},{32,72},{40,80},{48,88},{56,96},{64,... | collective-permute-start | bytes 196616 | tf_op jit(solution)/shard_map/ppermute | solution.py:18
  23.6 0.8 copy-done.1
  24.8 0.6 copy-done.4
  26.0 0.8 dynamic_slice.35
  26.8 3.8 %collective-permute-start.4 = (bf16[2,128,128]{2,1,0:T(8,128)(2,1)S(1)}, bf16[2,128,128]{2,1,0:T(8,128)(2,1)S(1)}, u32[]{:S(2)}, u32[]{:S(2)}) collective-permute-start(bf16[2,128,128]{2,1,0:T(8,128)(2,1)S(1)} %bitcast.175), channel_id=1, source_target_pairs={{0,8},{8,16},{16,24},{24,32},{32,40},{40,48},{48,56},{56,64},{64,7... | collective-permute-start | bytes 196616 | tf_op jit(solution)/shard_map/ppermute | solution.py:18
  30.6 6.4 %collective-permute-start.3 = (bf16[2,128,128]{2,1,0:T(8,128)(2,1)S(1)}, bf16[2,128,128]{2,1,0:T(8,128)(2,1)S(1)}, u32[]{:S(2)}, u32[]{:S(2)}) collective-permute-start(bf16[2,128,128]{2,1,0:T(8,128)(2,1)S(1)} %bitcast.176), channel_id=1, source_target_pairs={{0,16},{8,24},{16,32},{24,40},{32,48},{40,56},{48,64},{56,72},{64,... | collective-permute-start | bytes 196616 | tf_op jit(solution)/shard_map/ppermute | solution.py:18
  37.0 6.5 %collective-permute-start.2 = (bf16[2,128,128]{2,1,0:T(8,128)(2,1)S(1)}, bf16[2,128,128]{2,1,0:T(8,128)(2,1)S(1)}, u32[]{:S(2)}, u32[]{:S(2)}) collective-permute-start(bf16[2,128,128]{2,1,0:T(8,128)(2,1)S(1)} %bitcast.177), channel_id=1, source_target_pairs={{0,24},{8,32},{16,40},{24,48},{32,56},{40,64},{48,72},{56,80},{64,... | collective-permute-start | bytes 196616 | tf_op jit(solution)/shard_map/ppermute | solution.py:18
  43.5 9.1 %collective-permute-start.1 = (bf16[2,128,128]{2,1,0:T(8,128)(2,1)S(1)}, bf16[2,128,128]{2,1,0:T(8,128)(2,1)S(1)}, u32[]{:S(2)}, u32[]{:S(2)}) collective-permute-start(bf16[2,128,128]{2,1,0:T(8,128)(2,1)S(1)} %bitcast.178), channel_id=1, source_target_pairs={{0,32},{8,40},{16,48},{24,56},{32,64},{40,72},{48,80},{56,88},{64,... | collective-permute-start | bytes 196616 | tf_op jit(solution)/shard_map/ppermute | solution.py:18
  52.7 2.0 %collective-permute-done.1 = bf16[2,128,128]{2,1,0:T(8,128)(2,1)S(1)} collective-permute-done((bf16[2,128,128]{2,1,0:T(8,128)(2,1)S(1)}, bf16[2,128,128]{2,1,0:T(8,128)(2,1)S(1)}, u32[]{:S(2)}, u32[]{:S(2)}) %collective-permute-start.1) | collective-permute-done | bytes 65568 | tf_op jit(solution)/shard_map/ppermute | solution.py:18
  55.5 4.6 %while.29 = (s32[]{:T(128)}, f32[1,1,128,1,8,128]{2,5,4,3,1,0:T(8,128)S(1)}, f32[1,2,768,128]{3,2,1,0:T(8,128)S(1)}, s32[]{:T(128)}, s32[1]{0:T(128)}, /*index=5...) while((s32[]{:T(128)}, ...), condition=%wide.region_2.3_spmd.clone.clone, body=%wide.region_0.2_spmd.clone.clone.sunk | while | flops 169214240 | bytes 5122993 | solution.py:106
  56.9 0.6 and_reduce_fusion.2
  58.6 0.9 fusion.55
  60.2 15.0 %collective-permute-start.5 = (f32[2,128,128]{2,1,0:T(8,128)S(1)}, f32[2,128,128]{2,1,0:T(8,128)S(1)}, u32[]{:S(2)}, u32[]{:S(2)}) collective-permute-start(f32[2,128,128]{2,1,0:T(8,128)S(1)} %get-tuple-element.543), channel_id=1, source_target_pairs={{8,0},{16,8},{24,16},{32,24},{40,32},{48,40},{56,48},{64,56},{72,6... | collective-permute-start | bytes 393224 | tf_op jit(solution)/shard_map/ppermute | solution.py:18
  75.2 5.4 %collective-permute-start.9 = (f32[2,128,128]{2,1,0:T(8,128)S(1)}, f32[2,128,128]{2,1,0:T(8,128)S(1)}, u32[]{:S(2)}, u32[]{:S(2)}) collective-permute-start(f32[2,128,128]{2,1,0:T(8,128)S(1)} %get-tuple-element.544), channel_id=1, source_target_pairs={{40,0},{48,8},{56,16},{64,24},{72,32},{80,40},{88,48},{96,56},{104... | collective-permute-start | bytes 393224 | tf_op jit(solution)/shard_map/ppermute | solution.py:18
  80.7 17.7 %collective-permute-start.8 = (f32[2,128,128]{2,1,0:T(8,128)S(1)}, f32[2,128,128]{2,1,0:T(8,128)S(1)}, u32[]{:S(2)}, u32[]{:S(2)}) collective-permute-start(f32[2,128,128]{2,1,0:T(8,128)S(1)} %get-tuple-element.545), channel_id=1, source_target_pairs={{32,0},{40,8},{48,16},{56,24},{64,32},{72,40},{80,48},{88,56},{96,... | collective-permute-start | bytes 393224 | tf_op jit(solution)/shard_map/ppermute | solution.py:18
  98.4 2.5 %collective-permute-start.7 = (f32[2,128,128]{2,1,0:T(8,128)S(1)}, f32[2,128,128]{2,1,0:T(8,128)S(1)}, u32[]{:S(2)}, u32[]{:S(2)}) collective-permute-start(f32[2,128,128]{2,1,0:T(8,128)S(1)} %get-tuple-element.546), channel_id=1, source_target_pairs={{24,0},{32,8},{40,16},{48,24},{56,32},{64,40},{72,48},{80,56},{88,... | collective-permute-start | bytes 393224 | tf_op jit(solution)/shard_map/ppermute | solution.py:18
  100.9 5.6 %collective-permute-start.6 = (f32[2,128,128]{2,1,0:T(8,128)S(1)}, f32[2,128,128]{2,1,0:T(8,128)S(1)}, u32[]{:S(2)}, u32[]{:S(2)}) collective-permute-start(f32[2,128,128]{2,1,0:T(8,128)S(1)} %get-tuple-element.547), channel_id=1, source_target_pairs={{16,0},{24,8},{32,16},{40,24},{48,32},{56,40},{64,48},{72,56},{80,... | collective-permute-start | bytes 393224 | tf_op jit(solution)/shard_map/ppermute | solution.py:18
  106.5 0.9 copy.44
  107.4 2.1 %collective-permute-done.8 = f32[2,128,128]{2,1,0:T(8,128)S(1)} collective-permute-done((f32[2,128,128]{2,1,0:T(8,128)S(1)}, f32[2,128,128]{2,1,0:T(8,128)S(1)}, u32[]{:S(2)}, u32[]{:S(2)}) %collective-permute-start.8) | collective-permute-done | bytes 131104 | tf_op jit(solution)/shard_map/ppermute | solution.py:18
  109.5 4.8 %collective-permute-done.7 = f32[2,128,128]{2,1,0:T(8,128)S(1)} collective-permute-done((f32[2,128,128]{2,1,0:T(8,128)S(1)}, f32[2,128,128]{2,1,0:T(8,128)S(1)}, u32[]{:S(2)}, u32[]{:S(2)}) %collective-permute-start.7) | collective-permute-done | bytes 131104 | tf_op jit(solution)/shard_map/ppermute | solution.py:18
  114.3 6.1 %collective-permute-done.6 = f32[2,128,128]{2,1,0:T(8,128)S(1)} collective-permute-done((f32[2,128,128]{2,1,0:T(8,128)S(1)}, f32[2,128,128]{2,1,0:T(8,128)S(1)}, u32[]{:S(2)}, u32[]{:S(2)}) %collective-permute-start.6) | collective-permute-done | bytes 131104 | tf_op jit(solution)/shard_map/ppermute | solution.py:18
  120.4 0.6 slice_bitcast_fusion
  (42 shorter events, 5.0 us)
Async XLA Ops:
  12.4 10.8 %copy-start = (bf16[128,1024]{1,0:T(8,128)(2,1)S(1)}, bf16[128,1024]{1,0:T(8,128)(2,1)}, u32[]{:S(2)}) copy-start(bf16[128,1024]{1,0:T(8,128)(2,1)} %param.32) | copy-start | bytes 786436
  12.8 39.8 %collective-permute-start = (bf16[2,128,128]{2,1,0:T(8,128)(2,1)S(1)}, bf16[2,128,128]{2,1,0:T(8,128)(2,1)S(1)}, u32[]{:S(2)}, u32[]{:S(2)}) collective-permute-start(bf16[2,128,128]{2,1,0:T(8,128)(2,1)S(1)} %bitcast.174), channel_id=1, source_target_pairs={{0,40},{8,48},{16,56},{24,64},{32,72},{40,80},{48,88},{56,96},{64,... | collective-permute-start | bytes 196616 | tf_op jit(solution)/shard_map/ppermute | solution.py:18
  23.4 1.0 copy-start.1
  24.8 0.7 copy-start.4
  26.8 28.0 %collective-permute-start.4 = (bf16[2,128,128]{2,1,0:T(8,128)(2,1)S(1)}, bf16[2,128,128]{2,1,0:T(8,128)(2,1)S(1)}, u32[]{:S(2)}, u32[]{:S(2)}) collective-permute-start(bf16[2,128,128]{2,1,0:T(8,128)(2,1)S(1)} %bitcast.175), channel_id=1, source_target_pairs={{0,8},{8,16},{16,24},{24,32},{32,40},{40,48},{48,56},{56,64},{64,7... | collective-permute-start | bytes 196616 | tf_op jit(solution)/shard_map/ppermute | solution.py:18
  30.6 24.1 %collective-permute-start.3 = (bf16[2,128,128]{2,1,0:T(8,128)(2,1)S(1)}, bf16[2,128,128]{2,1,0:T(8,128)(2,1)S(1)}, u32[]{:S(2)}, u32[]{:S(2)}) collective-permute-start(bf16[2,128,128]{2,1,0:T(8,128)(2,1)S(1)} %bitcast.176), channel_id=1, source_target_pairs={{0,16},{8,24},{16,32},{24,40},{32,48},{40,56},{48,64},{56,72},{64,... | collective-permute-start | bytes 196616 | tf_op jit(solution)/shard_map/ppermute | solution.py:18
  37.0 17.7 %collective-permute-start.2 = (bf16[2,128,128]{2,1,0:T(8,128)(2,1)S(1)}, bf16[2,128,128]{2,1,0:T(8,128)(2,1)S(1)}, u32[]{:S(2)}, u32[]{:S(2)}) collective-permute-start(bf16[2,128,128]{2,1,0:T(8,128)(2,1)S(1)} %bitcast.177), channel_id=1, source_target_pairs={{0,24},{8,32},{16,40},{24,48},{32,56},{40,64},{48,72},{56,80},{64,... | collective-permute-start | bytes 196616 | tf_op jit(solution)/shard_map/ppermute | solution.py:18
  43.5 11.1 %collective-permute-start.1 = (bf16[2,128,128]{2,1,0:T(8,128)(2,1)S(1)}, bf16[2,128,128]{2,1,0:T(8,128)(2,1)S(1)}, u32[]{:S(2)}, u32[]{:S(2)}) collective-permute-start(bf16[2,128,128]{2,1,0:T(8,128)(2,1)S(1)} %bitcast.178), channel_id=1, source_target_pairs={{0,32},{8,40},{16,48},{24,56},{32,64},{40,72},{48,80},{56,88},{64,... | collective-permute-start | bytes 196616 | tf_op jit(solution)/shard_map/ppermute | solution.py:18
  54.8 0.7 copy-start.2
  54.8 0.7 copy-start.3
  60.2 47.1 %collective-permute-start.5 = (f32[2,128,128]{2,1,0:T(8,128)S(1)}, f32[2,128,128]{2,1,0:T(8,128)S(1)}, u32[]{:S(2)}, u32[]{:S(2)}) collective-permute-start(f32[2,128,128]{2,1,0:T(8,128)S(1)} %get-tuple-element.543), channel_id=1, source_target_pairs={{8,0},{16,8},{24,16},{32,24},{40,32},{48,40},{56,48},{64,56},{72,6... | collective-permute-start | bytes 393224 | tf_op jit(solution)/shard_map/ppermute | solution.py:18
  75.2 32.1 %collective-permute-start.9 = (f32[2,128,128]{2,1,0:T(8,128)S(1)}, f32[2,128,128]{2,1,0:T(8,128)S(1)}, u32[]{:S(2)}, u32[]{:S(2)}) collective-permute-start(f32[2,128,128]{2,1,0:T(8,128)S(1)} %get-tuple-element.544), channel_id=1, source_target_pairs={{40,0},{48,8},{56,16},{64,24},{72,32},{80,40},{88,48},{96,56},{104... | collective-permute-start | bytes 393224 | tf_op jit(solution)/shard_map/ppermute | solution.py:18
  80.7 28.8 %collective-permute-start.8 = (f32[2,128,128]{2,1,0:T(8,128)S(1)}, f32[2,128,128]{2,1,0:T(8,128)S(1)}, u32[]{:S(2)}, u32[]{:S(2)}) collective-permute-start(f32[2,128,128]{2,1,0:T(8,128)S(1)} %get-tuple-element.545), channel_id=1, source_target_pairs={{32,0},{40,8},{48,16},{56,24},{64,32},{72,40},{80,48},{88,56},{96,... | collective-permute-start | bytes 393224 | tf_op jit(solution)/shard_map/ppermute | solution.py:18
  98.4 15.9 %collective-permute-start.7 = (f32[2,128,128]{2,1,0:T(8,128)S(1)}, f32[2,128,128]{2,1,0:T(8,128)S(1)}, u32[]{:S(2)}, u32[]{:S(2)}) collective-permute-start(f32[2,128,128]{2,1,0:T(8,128)S(1)} %get-tuple-element.546), channel_id=1, source_target_pairs={{24,0},{32,8},{40,16},{48,24},{56,32},{64,40},{72,48},{80,56},{88,... | collective-permute-start | bytes 393224 | tf_op jit(solution)/shard_map/ppermute | solution.py:18
  100.9 19.5 %collective-permute-start.6 = (f32[2,128,128]{2,1,0:T(8,128)S(1)}, f32[2,128,128]{2,1,0:T(8,128)S(1)}, u32[]{:S(2)}, u32[]{:S(2)}) collective-permute-start(f32[2,128,128]{2,1,0:T(8,128)S(1)} %get-tuple-element.547), channel_id=1, source_target_pairs={{16,0},{24,8},{32,16},{40,24},{48,32},{56,40},{64,48},{72,56},{80,... | collective-permute-start | bytes 393224 | tf_op jit(solution)/shard_map/ppermute | solution.py:18
where the time goes:
time: 123 us; the launch traced here: 121 us
  starting transfers between devices  82.5 us (67%)
  waiting for transfers between devices  15 us (12%)
  blocking collectives  9.72 us (8%)
  local copies, waits for them, and re-layouts  7.5 us (6%)
  loops' own time  2.02 us (2%)
  matrix products  1.8 us (1%)
  other arithmetic  1.59 us (1%)
    ppermute x10, starting transfers between devices, from_behind(): lax.ppermute(value, axis, [(source, source + steps) for source in range(i...  82.5 us
    ppermute x10, waiting for transfers between devices, from_behind(): lax.ppermute(value, axis, [(source, source + steps) for source in range(i...  15 us
    all_to_all x1, blocking collectives, per_device(): lax.all_to_all(jnp.stack([keys, values]), 'head', split_axis=2, concat_ax...  9.72 us
    unnamed x21, local copies, waits for them, and re-layouts  3.73 us
  transfers between devices with their start and end apart: 10, of which 4 were waited for; matrix products, arithmetic and copies ran while one was open for 2% of the time, Pallas kernels for 0%

commit v1 on v0

v1 whole, which is shorter than its diff:
```python
import functools
import math

import jax
import jax.numpy as jnp
from jax import lax
from jax.experimental import pallas as pl
from jax.experimental.pallas import tpu as pltpu
from jax.sharding import PartitionSpec as P

HEADS = 64
KV_HEADS = 8
HEAD_DIM = 128
QBLOCK = 128
REACH = 5
GROUP = HEADS // KV_HEADS
PIECES = 2
MESH = pl.DeviceIdType.MESH
FAR = 1 << 30

NT = (((1,), (1,)), ((), ()))
NN = (((1,), (0,)), ((), ()))


def matmul(a, b, dims):
    return lax.dot_general(a, b, dims, preferred_element_type=jnp.float32)


def kernel(
    n_tok,
    n_head,
    query_hbm,
    keys_hbm,
    values_hbm,
    outgrad_hbm,
    norm_hbm,
    dot_hbm,
    starts_hbm,
    spans_hbm,
    dq_hbm,
    dk_hbm,
    dv_hbm,
    q_s,
    do_s,
    norm_s,
    dot_s,
    starts_s,
    spans_s,
    key_win,
    value_win,
    key_t,
    ds_all,
    send_buf,
    recv_buf,
    own_buf,
    far_buf,
    dq_s,
    out_s,
    in_sem,
    a2a_send,
    own_sem,
    kv_send,
    kv_recv,
    grad_send,
    grad_recv,
    out_sem,
):
    scale = 1.0 / math.sqrt(HEAD_DIM)
    tok = lax.axis_index("tok")
    head = lax.axis_index("head")
    rows = QBLOCK // n_head
    half = QBLOCK // PIECES

    def tok_at(step):
        return lax.rem(tok + (step + n_tok), n_tok)

    slot_rows = pl.ds(pl.multiple_of(head * rows, rows), rows)
    my_half = lax.div(head, n_head // PIECES)

    def columns(h):
        return pl.ds(pl.multiple_of(h * HEAD_DIM, HEAD_DIM), HEAD_DIM)

    own_copies = []
    for side, (source, window) in enumerate(((keys_hbm, key_win), (values_hbm, value_win))):
        own_copies.append(
            pltpu.make_async_copy(
                source.at[:, columns(head)], window.at[0, slot_rows, :], own_sem.at[side, my_half]
            )
        )
    for copy in own_copies:
        copy.start()
    loads = []
    for h in range(GROUP):
        block = pl.ds(h * QBLOCK, QBLOCK)
        cols = pl.ds(h * HEAD_DIM, HEAD_DIM)
        loads.append(pltpu.make_async_copy(query_hbm.at[:, cols], q_s.at[block, :], in_sem.at[h]))
        loads.append(
            pltpu.make_async_copy(outgrad_hbm.at[:, cols], do_s.at[block, :], in_sem.at[GROUP + h])
        )
    base = 2 * GROUP
    loads.append(pltpu.make_async_copy(norm_hbm, norm_s, in_sem.at[base]))
    loads.append(pltpu.make_async_copy(dot_hbm, dot_s, in_sem.at[base + 1]))
    loads.append(pltpu.make_async_copy(starts_hbm, starts_s, in_sem.at[base + 2]))
    loads.append(pltpu.make_async_copy(spans_hbm, spans_s, in_sem.at[base + 3]))
    for copy in loads:
        copy.start()

    barrier = pltpu.get_barrier_semaphore()
    for step in range(1, n_head):
        pl.semaphore_signal(
            barrier, 1, device_id={"head": lax.rem(head + step, n_head)}, device_id_type=MESH
        )
    for step in (1, -1):
        pl.semaphore_signal(barrier, 1, device_id={"tok": tok_at(step)}, device_id_type=MESH)
    pl.semaphore_wait(barrier, n_head + 1)

    spreads = []
    for side, (source, window) in enumerate(((keys_hbm, key_win), (values_hbm, value_win))):
        for step in range(1, n_head):
            peer = lax.rem(head + step, n_head)
            copy = pltpu.make_async_remote_copy(
                src_ref=source.at[:, columns(peer)],
                dst_ref=window.at[0, slot_rows, :],
                send_sem=a2a_send.at[side, step - 1],
                recv_sem=own_sem.at[side, my_half],
                device_id={"head": peer},
                device_id_type=MESH,
            )
            copy.start()
            spreads.append(copy)

    def piece(slot, side, part):
        window = (key_win, value_win)[side]
        return window.at[slot, pl.ds(part * half, half), :]

    forwards = []

    def forward(slot, side, part):
        copy = pltpu.make_async_remote_copy(
            src_ref=piece(slot, side, part),
            dst_ref=piece(slot + 1, side, part),
            send_sem=kv_send.at[slot, side, part],
            recv_sem=kv_recv.at[slot, side, part],
            device_id={"tok": tok_at(1)},
            device_id_type=MESH,
        )
        copy.start()
        forwards.append(copy)
        return copy

    for side in range(2):
        for part in range(PIECES):
            view = piece(0, side, part)
            pltpu.make_async_copy(view, view, own_sem.at[side, part]).wait()
            forward(0, side, part)
    for copy in loads:
        copy.wait()

    start_row = starts_s[pl.ds(tok, 1), :]
    span = spans_s[tok]
    row_iota = lax.broadcasted_iota(jnp.int32, (QBLOCK, QBLOCK), 0)
    col_iota = lax.broadcasted_iota(jnp.int32, (QBLOCK, QBLOCK), 1)

    def block(slot):
        key = key_win[slot]
        value = value_win[slot]
        key_pos = row_iota + (tok - slot) * QBLOCK
        least = jnp.where(slot < span, start_row, FAR)
        allowed = key_pos >= least
        if slot == 0:
            allowed = allowed & (row_iota <= col_iota)
        value_term = jnp.zeros((QBLOCK, HEAD_DIM), jnp.float32)
        key_term = jnp.zeros((QBLOCK, HEAD_DIM), jnp.float32)
        for pair in range(GROUP // 2):
            block_rows = pl.ds(pair * 2 * QBLOCK, 2 * QBLOCK)
            q_pair = q_s[block_rows, :]
            do_pair = do_s[block_rows, :]
            scores = matmul(key, q_pair, NT)
            prob_grad = matmul(value, do_pair, NT)
            lows, grads = [], []
            for e in range(2):
                h = pair * 2 + e
                lanes = slice(e * QBLOCK, (e + 1) * QBLOCK)
                probs = jnp.where(
                    allowed, jnp.exp(scores[:, lanes] * scale - norm_s[pl.ds(h, 1), :]), 0.0
                )
                lows.append(probs.astype(jnp.bfloat16))
                grads.append(
                    (probs * (prob_grad[:, lanes] - dot_s[pl.ds(h, 1), :])).astype(jnp.bfloat16)
                )
            low = jnp.concatenate(lows, axis=1)
            grad = jnp.concatenate(grads, axis=1)
            ds_all[slot, :, pl.ds(pair * 2 * QBLOCK, 2 * QBLOCK)] = grad
            value_term = value_term + matmul(low, do_pair, NN)
            key_term = key_term + matmul(grad, q_pair, NN)
        key_t[:, pl.ds(slot * QBLOCK, QBLOCK)] = key.T
        return key_term * scale, value_term

    grad_sends = []

    def send_grad(slot, side, step):
        copy = pltpu.make_async_remote_copy(
            src_ref=send_buf.at[slot, side],
            dst_ref=recv_buf.at[slot, side],
            send_sem=grad_send.at[slot, side],
            recv_sem=grad_recv.at[slot, side],
            device_id={"tok": tok_at(-step)},
            device_id_type=MESH,
        )
        copy.start()
        grad_sends.append(copy)
        return copy

    key_term, value_term = block(0)
    own_buf[0] = key_term
    own_buf[1] = value_term
    grads = {}
    for slot in range(1, REACH + 1):
        for side in range(2):
            for part in range(PIECES):
                forwards[((slot - 1) * 2 + side) * PIECES + part].wait_recv()
                if slot < REACH:
                    forward(slot, side, part)
        key_term, value_term = block(slot)
        if slot == REACH - 1:
            far_buf[0] = key_term
            far_buf[1] = value_term
        else:
            send_buf[slot - 1, 0] = key_term.astype(jnp.bfloat16)
            send_buf[slot - 1, 1] = value_term.astype(jnp.bfloat16)
            for side in range(2):
                grads[slot, side] = send_grad(slot - 1, side, 1 if slot == REACH else slot)

    outs = []
    for pair in range(GROUP // 2):
        lanes = pl.ds(pair * 2 * QBLOCK, 2 * QBLOCK)
        grad = ds_all[:, :, lanes].reshape((REACH + 1) * QBLOCK, 2 * QBLOCK)
        dq_t = matmul(key_t[...], grad, NN) * scale
        for e in range(2):
            h = pair * 2 + e
            dq_s[:, pl.ds(h * HEAD_DIM, HEAD_DIM)] = (
                dq_t[:, e * QBLOCK : (e + 1) * QBLOCK].T.astype(jnp.bfloat16)
            )

    for side in range(2):
        grads[REACH, side].wait_recv()
        send_buf[REACH - 2, side] = (
            far_buf[side] + recv_buf[REACH - 1, side].astype(jnp.float32)
        ).astype(jnp.bfloat16)
        grads[REACH - 1, side] = send_grad(REACH - 2, side, REACH - 1)
    copy = pltpu.make_async_copy(dq_s, dq_hbm, out_sem.at[0])
    copy.start()
    outs.append(copy)
    for side in range(2):
        total = own_buf[side]
        for slot in range(1, REACH):
            grads[slot, side].wait_recv()
            total = total + recv_buf[slot - 1, side].astype(jnp.float32)
        out_s[side] = total.astype(jnp.bfloat16)
        copy = pltpu.make_async_copy(out_s.at[side], (dk_hbm, dv_hbm)[side], out_sem.at[1 + side])
        copy.start()
        outs.append(copy)
    for copy in own_copies:
        pass
    for copy in spreads:
        copy.wait_send()
    for copy in forwards:
        copy.wait_send()
    for copy in grad_sends:
        copy.wait_send()
    for copy in outs:
        copy.wait()


def solution(mesh):
    n_tok = mesh.shape["tok"]
    n_head = mesh.shape["head"]
    slots = REACH + 1
    bf16, f32 = jnp.bfloat16, jnp.float32

    def per_device(query, keys, values, out_grad, log_norm, row_dot, doc_start, spans):
        starts = doc_start.reshape(n_tok, QBLOCK)
        anywhere = pl.BlockSpec(memory_space=pl.ANY)
        return pl.pallas_call(
            functools.partial(kernel, n_tok, n_head),
            out_shape=(
                jax.ShapeDtypeStruct((QBLOCK, GROUP * HEAD_DIM), bf16),
                jax.ShapeDtypeStruct((QBLOCK, HEAD_DIM), bf16),
                jax.ShapeDtypeStruct((QBLOCK, HEAD_DIM), bf16),
            ),
            in_specs=[anywhere] * 8,
            out_specs=(anywhere,) * 3,
            scratch_shapes=[
                pltpu.VMEM((GROUP * QBLOCK, HEAD_DIM), bf16),
                pltpu.VMEM((GROUP * QBLOCK, HEAD_DIM), bf16),
                pltpu.VMEM((GROUP, QBLOCK), f32),
                pltpu.VMEM((GROUP, QBLOCK), f32),
                pltpu.VMEM((n_tok, QBLOCK), jnp.int32),
                pltpu.SMEM((n_tok,), jnp.int32),
                pltpu.VMEM((slots, QBLOCK, HEAD_DIM), bf16),
                pltpu.VMEM((slots, QBLOCK, HEAD_DIM), bf16),
                pltpu.VMEM((HEAD_DIM, slots * QBLOCK), bf16),
                pltpu.VMEM((slots, QBLOCK, GROUP * QBLOCK), bf16),
                pltpu.VMEM((REACH, 2, QBLOCK, HEAD_DIM), bf16),
                pltpu.VMEM((REACH, 2, QBLOCK, HEAD_DIM), bf16),
                pltpu.VMEM((2, QBLOCK, HEAD_DIM), f32),
                pltpu.VMEM((2, QBLOCK, HEAD_DIM), f32),
                pltpu.VMEM((QBLOCK, GROUP * HEAD_DIM), bf16),
                pltpu.VMEM((2, QBLOCK, HEAD_DIM), bf16),
                pltpu.SemaphoreType.DMA((2 * GROUP + 4,)),
                pltpu.SemaphoreType.DMA((2, n_head - 1)),
                pltpu.SemaphoreType.DMA((2, PIECES)),
                pltpu.SemaphoreType.DMA((REACH, 2, PIECES)),
                pltpu.SemaphoreType.DMA((REACH, 2, PIECES)),
                pltpu.SemaphoreType.DMA((REACH, 2)),
                pltpu.SemaphoreType.DMA((REACH, 2)),
                pltpu.SemaphoreType.DMA((3,)),
            ],
            compiler_params=pltpu.CompilerParams(collective_id=0, has_side_effects=True),
        )(query, keys, values, out_grad, log_norm, row_dot, starts, spans)

    return jax.shard_map(
        per_device,
        mesh=mesh,
        in_specs=(
            P("tok", "head"),
            P(("tok", "head"), None),
            P(("tok", "head"), None),
            P("tok", "head"),
            P("head", "tok"),
            P("head", "tok"),
            P(),
            P(),
        ),
        out_specs=(P("tok", "head"), P("tok", "head"), P("tok", "head")),
        check_vma=False,
    )
```

time: 123 us -> 53.5 us (0.43)
  the two profiles are of different devices: /device:TPU:24 before, /device:TPU:2 now
where the time goes in v1:
time: 53.5 us; the launch traced here: 53.3 us
  Pallas kernels  49.6 us (93%)
  local copies, waits for them, and re-layouts  3.06 us (6%)
  between operations  0.65 us (1%)
    pallas_call x1, Pallas kernels, per_device(): pl.pallas_call(functools.partial(kernel, n_tok, n_head), out_shape=(jax.S...  49.6 us
    unnamed x7, local copies, waits for them, and re-layouts  3.06 us

profile of v1, /device:TPU:2, one launch (start us, length us, event | category | flops | bytes accessed | tf_op | source)
XLA Modules:
  0.0 53.3 jit_solution(8225000389944466032)
XLA Ops:
  0.6 49.6 %shard_map.103 = (bf16[128,1024]{1,0:T(8,128)(2,1)}, bf16[128,128]{1,0:T(8,128)(2,1)}, bf16[128,128]{1,0:T(8,128)(2,1)}) custom-call(bf16[128,1024]{1,0:T(8,128)(2,1)} %query_hbm.1, bf16[16,1024]{1,0:T(8,128)(2,1)} %keys_hbm.1, bf16[16,1024]{1,0:T(8,128)(2,1)} %values_hbm.1, bf16[128,1024]{1,0:T(8,128)(2,1)} %outgrad_hbm.1, f32[8,128]{1,0:T(8,128)} %norm_hbm.1, ...), custom_call_target="tpu_custom_call" | custom-call | tf_op jit(solution)/shard_map/pallas_call | solution.py:284
  50.2 0.0 copy-start.1
  50.2 1.7 %copy.14 = bf16[128,1024]{1,0:T(8,128)(2,1)} copy(bf16[128,1024]{1,0:T(8,128)(2,1)} %get-tuple-element.6) | data formatting | bytes 524288
  51.9 0.0 copy-done.1
  51.9 0.0 copy-start
  51.9 0.6 %copy.15 = bf16[128,128]{1,0:T(8,128)(2,1)} copy(bf16[128,128]{1,0:T(8,128)(2,1)S(1)} %copy-done.1) | data formatting | bytes 65536
  52.5 0.2 copy-done
  52.7 0.6 %copy.16 = bf16[128,128]{1,0:T(8,128)(2,1)} copy(bf16[128,128]{1,0:T(8,128)(2,1)S(1)} %copy-done) | data formatting | bytes 65536
Async XLA Ops:
  50.2 1.7 %copy-start.1 = (bf16[128,128]{1,0:T(8,128)(2,1)S(1)}, bf16[128,128]{1,0:T(8,128)(2,1)}, u32[]{:S(2)}) copy-start(bf16[128,128]{1,0:T(8,128)(2,1)} %get-tuple-element.7) | copy-start | bytes 98308
  51.9 0.8 %copy-start = (bf16[128,128]{1,0:T(8,128)(2,1)S(1)}, bf16[128,128]{1,0:T(8,128)(2,1)}, u32[]{:S(2)}) copy-start(bf16[128,128]{1,0:T(8,128)(2,1)} %get-tuple-element.8) | copy-start | bytes 98308

commit v2 on v1

v2 whole, which is shorter than its diff:
```python
import functools
import math

import jax
import jax.numpy as jnp
from jax import lax
from jax.experimental import pallas as pl
from jax.experimental.pallas import tpu as pltpu
from jax.sharding import PartitionSpec as P

HEADS = 64
KV_HEADS = 8
HEAD_DIM = 128
QBLOCK = 128
REACH = 5
GROUP = HEADS // KV_HEADS
PIECES = 2
MESH = pl.DeviceIdType.MESH
FAR = 1 << 30
NS = jax.named_scope

NT = (((1,), (1,)), ((), ()))
NN = (((1,), (0,)), ((), ()))


def matmul(a, b, dims):
    return lax.dot_general(a, b, dims, preferred_element_type=jnp.float32)


def kernel(
    n_tok,
    n_head,
    query_hbm,
    keys_hbm,
    values_hbm,
    outgrad_hbm,
    norm_hbm,
    dot_hbm,
    starts_hbm,
    spans_hbm,
    dq_out,
    dk_out,
    dv_out,
    q_s,
    do_s,
    norm_s,
    dot_s,
    starts_s,
    spans_s,
    key_win,
    value_win,
    key_t,
    ds_all,
    send_buf,
    recv_buf,
    terms,
    in_sem,
    a2a_send,
    own_sem,
    kv_send,
    kv_recv,
    grad_send,
    grad_recv,
):
    scale = 1.0 / math.sqrt(HEAD_DIM)
    tok = lax.axis_index("tok")
    head = lax.axis_index("head")
    rows = QBLOCK // n_head
    half = QBLOCK // PIECES

    def tok_at(step):
        return lax.rem(tok + (step + n_tok), n_tok)

    slot_rows = pl.ds(pl.multiple_of(head * rows, rows), rows)
    my_half = lax.div(head, n_head // PIECES)

    def columns(h):
        return pl.ds(pl.multiple_of(h * HEAD_DIM, HEAD_DIM), HEAD_DIM)

    barrier = pltpu.get_barrier_semaphore()
    for step in range(1, n_head):
        pl.semaphore_signal(
            barrier, 1, device_id={"head": lax.rem(head + step, n_head)}, device_id_type=MESH
        )
    pl.semaphore_signal(barrier, 1, device_id={"tok": tok_at(-1)}, device_id_type=MESH)

    for side, (source, window) in enumerate(((keys_hbm, key_win), (values_hbm, value_win))):
        pltpu.make_async_copy(
            source.at[:, columns(head)], window.at[0, slot_rows, :], own_sem.at[side, my_half]
        ).start()
    loads = []
    for h in range(GROUP):
        block = pl.ds(h * QBLOCK, QBLOCK)
        cols = pl.ds(h * HEAD_DIM, HEAD_DIM)
        loads.append(pltpu.make_async_copy(query_hbm.at[:, cols], q_s.at[block, :], in_sem.at[h]))
        loads.append(
            pltpu.make_async_copy(outgrad_hbm.at[:, cols], do_s.at[block, :], in_sem.at[GROUP + h])
        )
    base = 2 * GROUP
    loads.append(pltpu.make_async_copy(norm_hbm, norm_s, in_sem.at[base]))
    loads.append(pltpu.make_async_copy(dot_hbm, dot_s, in_sem.at[base + 1]))
    loads.append(pltpu.make_async_copy(starts_hbm, starts_s, in_sem.at[base + 2]))
    loads.append(pltpu.make_async_copy(spans_hbm, spans_s, in_sem.at[base + 3]))
    for copy in loads:
        copy.start()
    with NS("xbar"):
        pl.semaphore_wait(barrier, n_head)

    spreads = []
    for side, (source, window) in enumerate(((keys_hbm, key_win), (values_hbm, value_win))):
        for step in range(1, n_head):
            peer = lax.rem(head + step, n_head)
            copy = pltpu.make_async_remote_copy(
                src_ref=source.at[:, columns(peer)],
                dst_ref=window.at[0, slot_rows, :],
                send_sem=a2a_send.at[side, step - 1],
                recv_sem=own_sem.at[side, my_half],
                device_id={"head": peer},
                device_id_type=MESH,
            )
            copy.start()
            spreads.append(copy)

    def piece(slot, side, part):
        window = (key_win, value_win)[side]
        return window.at[slot, pl.ds(part * half, half), :]

    forwards = {}

    def forward(slot, side, part):
        copy = pltpu.make_async_remote_copy(
            src_ref=piece(slot, side, part),
            dst_ref=piece(slot + 1, side, part),
            send_sem=kv_send.at[slot, side, part],
            recv_sem=kv_recv.at[slot, side, part],
            device_id={"tok": tok_at(1)},
            device_id_type=MESH,
        )
        copy.start()
        forwards[slot, side, part] = copy

    pieces = [(side, part) for side in range(2) for part in range(PIECES)]
    for side, part in pieces:
        view = piece(0, side, part)
        with NS(f"xa2a{side}{part}"):
            pltpu.make_async_copy(view, view, own_sem.at[side, part]).wait()
        forward(0, side, part)
    with NS("xloads"):
        for copy in loads:
            copy.wait()

    start_row = starts_s[pl.ds(tok, 1), :]
    span = spans_s[tok]
    row_iota = lax.broadcasted_iota(jnp.int32, (QBLOCK, QBLOCK), 0)
    col_iota = lax.broadcasted_iota(jnp.int32, (QBLOCK, QBLOCK), 1)

    def unit(slot, pair):
        key = key_win[slot]
        value = value_win[slot]
        key_pos = row_iota + (tok - slot) * QBLOCK
        least = jnp.where(slot < span, start_row, FAR)
        allowed = key_pos >= least
        if slot == 0:
            allowed = allowed & (row_iota <= col_iota)
        block_rows = pl.ds(pair * 2 * QBLOCK, 2 * QBLOCK)
        q_pair = q_s[block_rows, :]
        do_pair = do_s[block_rows, :]
        scores = matmul(key, q_pair, NT)
        prob_grad = matmul(value, do_pair, NT)
        lows, grads = [], []
        for e in range(2):
            h = pair * 2 + e
            lanes = slice(e * QBLOCK, (e + 1) * QBLOCK)
            probs = jnp.where(
                allowed, jnp.exp(scores[:, lanes] * scale - norm_s[pl.ds(h, 1), :]), 0.0
            )
            lows.append(probs.astype(jnp.bfloat16))
            grads.append(
                (probs * (prob_grad[:, lanes] - dot_s[pl.ds(h, 1), :])).astype(jnp.bfloat16)
            )
        low = jnp.concatenate(lows, axis=1)
        grad = jnp.concatenate(grads, axis=1)
        ds_all[slot, :, block_rows] = grad
        key_term = matmul(grad, q_pair, NN)
        value_term = matmul(low, do_pair, NN)
        if pair == 0:
            key_t[:, pl.ds(slot * QBLOCK, QBLOCK)] = key.T
            terms[slot, 0] = key_term
            terms[slot, 1] = value_term
        else:
            terms[slot, 0] += key_term
            terms[slot, 1] += value_term

    grads = {}

    def send_grad(slot, side, step, extra=None):
        term = terms[slot, side]
        if side == 0:
            term = term * scale
        if extra is not None:
            term = term + extra
        send_buf[slot - 1, side] = term.astype(jnp.bfloat16)
        copy = pltpu.make_async_remote_copy(
            src_ref=send_buf.at[slot - 1, side],
            dst_ref=recv_buf.at[slot - 1, side],
            send_sem=grad_send.at[slot - 1, side],
            recv_sem=grad_recv.at[slot - 1, side],
            device_id={"tok": tok_at(-step)},
            device_id_type=MESH,
        )
        copy.start()
        grads[slot, side] = copy

    def finish(slot):
        if slot % 2 == 1:
            for side in range(2):
                send_grad(slot, side, 1)

    def join(slot):
        for side in range(2):
            with NS(f"xjoin{slot}{side}"):
                grads[slot + 1, side].wait_recv()
            send_grad(slot, side, slot, recv_buf[slot, side].astype(jnp.float32))

    for slot in range(1, REACH + 1):
        for index, (side, part) in enumerate(pieces):
            with NS(f"xkv{slot}{side}{part}"):
                forwards[slot - 1, side, part].wait_recv()
            if slot < REACH:
                forward(slot, side, part)
            with NS(f"xunit{slot - 1}{index}"):
                unit(slot - 1, index)
        finish(slot - 1)
    with NS("xunit5"):
        for pair in range(GROUP // 2):
            unit(REACH, pair)
    finish(REACH)
    join(2)

    with NS("xdq"):
        for pair in range(GROUP // 2):
            lanes = pl.ds(pair * 2 * QBLOCK, 2 * QBLOCK)
            grad = ds_all[:, :, lanes].reshape((REACH + 1) * QBLOCK, 2 * QBLOCK)
            dq_t = matmul(key_t[...], grad, NN) * scale
            for e in range(2):
                h = pair * 2 + e
                dq_out[:, pl.ds(h * HEAD_DIM, HEAD_DIM)] = (
                    dq_t[:, e * QBLOCK : (e + 1) * QBLOCK].T.astype(jnp.bfloat16)
                )
    join(4)
    for side, out in enumerate((dk_out, dv_out)):
        total = terms[0, side]
        if side == 0:
            total = total * scale
        for slot in (1, 2, 4):
            with NS(f"xgrad{side}{slot}"):
                grads[slot, side].wait_recv()
            total = total + recv_buf[slot - 1, side].astype(jnp.float32)
        out[...] = total.astype(jnp.bfloat16)
    with NS("xsends"):
        for copy in spreads + list(forwards.values()) + list(grads.values()):
            copy.wait_send()


def store(dq_ref, dk_ref, dv_ref, dq_hbm, dk_hbm, dv_hbm, sems):
    copies = [
        pltpu.make_async_copy(source, target, sems.at[index])
        for index, (source, target) in enumerate(
            ((dq_ref, dq_hbm), (dk_ref, dk_hbm), (dv_ref, dv_hbm))
        )
    ]
    for copy in copies:
        copy.start()
    for copy in copies:
        copy.wait()


def solution(mesh):
    n_tok = mesh.shape["tok"]
    n_head = mesh.shape["head"]
    slots = REACH + 1
    bf16, f32 = jnp.bfloat16, jnp.float32

    def per_device(query, keys, values, out_grad, log_norm, row_dot, doc_start, spans):
        starts = doc_start.reshape(n_tok, QBLOCK)
        anywhere = pl.BlockSpec(memory_space=pl.ANY)
        outside = pl.BlockSpec(memory_space=pltpu.HBM)
        inside = pl.BlockSpec(memory_space=pltpu.VMEM)
        shapes = (
            jax.ShapeDtypeStruct((QBLOCK, GROUP * HEAD_DIM), bf16),
            jax.ShapeDtypeStruct((QBLOCK, HEAD_DIM), bf16),
            jax.ShapeDtypeStruct((QBLOCK, HEAD_DIM), bf16),
        )
        grads = pl.pallas_call(
            functools.partial(kernel, n_tok, n_head),
            out_shape=tuple(pltpu.VMEM(shape.shape, shape.dtype) for shape in shapes),
            in_specs=[outside] * 8,
            out_specs=(inside,) * 3,
            scratch_shapes=[
                pltpu.VMEM((GROUP * QBLOCK, HEAD_DIM), bf16),
                pltpu.VMEM((GROUP * QBLOCK, HEAD_DIM), bf16),
                pltpu.VMEM((GROUP, QBLOCK), f32),
                pltpu.VMEM((GROUP, QBLOCK), f32),
                pltpu.VMEM((n_tok, QBLOCK), jnp.int32),
                pltpu.SMEM((n_tok,), jnp.int32),
                pltpu.VMEM((slots, QBLOCK, HEAD_DIM), bf16),
                pltpu.VMEM((slots, QBLOCK, HEAD_DIM), bf16),
                pltpu.VMEM((HEAD_DIM, slots * QBLOCK), bf16),
                pltpu.VMEM((slots, QBLOCK, GROUP * QBLOCK), bf16),
                pltpu.VMEM((REACH, 2, QBLOCK, HEAD_DIM), bf16),
                pltpu.VMEM((REACH, 2, QBLOCK, HEAD_DIM), bf16),
                pltpu.VMEM((slots, 2, QBLOCK, HEAD_DIM), f32),
                pltpu.SemaphoreType.DMA((2 * GROUP + 4,)),
                pltpu.SemaphoreType.DMA((2, n_head - 1)),
                pltpu.SemaphoreType.DMA((2, PIECES)),
                pltpu.SemaphoreType.DMA((REACH, 2, PIECES)),
                pltpu.SemaphoreType.DMA((REACH, 2, PIECES)),
                pltpu.SemaphoreType.DMA((REACH, 2)),
                pltpu.SemaphoreType.DMA((REACH, 2)),
            ],
            compiler_params=pltpu.CompilerParams(
                collective_id=0, has_side_effects=True
            ),
        )(query, keys, values, out_grad, log_norm, row_dot, starts, spans)
        return pl.pallas_call(
            store,
            out_shape=shapes,
            in_specs=[inside] * 3,
            out_specs=(anywhere,) * 3,
            scratch_shapes=[pltpu.SemaphoreType.DMA((3,))],
            compiler_params=pltpu.CompilerParams(vmem_limit_bytes=4 << 20),
        )(*grads)

    return jax.shard_map(
        per_device,
        mesh=mesh,
        in_specs=(
            P("tok", "head"),
            P(("tok", "head"), None),
            P(("tok", "head"), None),
            P("tok", "head"),
            P("head", "tok"),
            P("head", "tok"),
            P(),
            P(),
        ),
        out_specs=(P("tok", "head"), P("tok", "head"), P("tok", "head")),
        check_vma=False,
    )
```

time: 53.5 us -> 50.5 us (0.944)
  the two profiles are of different devices: /device:TPU:2 before, /device:TPU:32 now
where the time goes in v2:
time: 50.5 us; the launch traced here: 50.4 us
  Pallas kernels  49.8 us (99%)
  between operations  0.64 us (1%)
    pallas_call x1, Pallas kernels, per_device(): pl.pallas_call(functools.partial(kernel, n_tok, n_head), out_shape=tuple(...  49 us

profile of v2, /device:TPU:32, one launch (start us, length us, event | category | flops | bytes accessed | tf_op | source)
XLA Modules:
  0.0 50.4 jit_solution(4223042298408098107)
XLA Ops:
  0.6 49.0 %shard_map.103 = (bf16[128,1024]{1,0:T(8,128)(2,1)S(1)}, bf16[128,128]{1,0:T(8,128)(2,1)S(1)}, bf16[128,128]{1,0:T(8,128)(2,1)S(1)}) custom-call(bf16[128,1024]{1,0:T(8,128)(2,1)} %query_hbm.1, bf16[16,1024]{1,0:T(8,128)(2,1)} %keys_hbm.1, bf16[16,1024]{1,0:T(8,128)(2,1)} %values_hbm.1, bf16[128,1024]{1,0:T(8,128)(2,1)} %outgrad_hbm.1, f32[8,128]{1,0:T(8,128)} %norm_hbm.1, ...), custom_call_target="tpu_custom_call" | custom-call | tf_op jit(solution)/shard_map/pallas_call | solution.py:294
  49.7 0.7 %shard_map.104 = (bf16[128,1024]{1,0:T(8,128)(2,1)}, bf16[128,128]{1,0:T(8,128)(2,1)}, bf16[128,128]{1,0:T(8,128)(2,1)}) custom-call(bf16[128,1024]{1,0:T(8,128)(2,1)S(1)} %get-tuple-element.6.dq_ref, bf16[128,128]{1,0:T(8,128)(2,1)S(1)} %get-tuple-element.7.dk_ref, bf16[128,128]{1,0:T(8,128)(2,1)S(1)} %get-tuple-element.8.dv_ref), custom_call_target="tpu_custom_call" | custom-call | tf_op jit(solution)/shard_map/pallas_call | solution.py:325

commit v3 on v2

v3 whole, which is shorter than its diff:
```python
import functools
import math

import jax
import jax.numpy as jnp
from jax import lax
from jax.experimental import pallas as pl
from jax.experimental.pallas import tpu as pltpu
from jax.sharding import PartitionSpec as P

HEADS = 64
KV_HEADS = 8
HEAD_DIM = 128
QBLOCK = 128
REACH = 5
GROUP = HEADS // KV_HEADS
PIECES = 2
MESH = pl.DeviceIdType.MESH
FAR = 1 << 30
NS = jax.named_scope
JOIN = 3
ROW = 32
SPLIT = True

NT = (((1,), (1,)), ((), ()))
NN = (((1,), (0,)), ((), ()))


def matmul(a, b, dims):
    return lax.dot_general(a, b, dims, preferred_element_type=jnp.float32)


def kernel(
    n_tok,
    n_head,
    query_hbm,
    keys_hbm,
    values_hbm,
    outgrad_hbm,
    norm_hbm,
    dot_hbm,
    starts_hbm,
    spans_hbm,
    dq_out,
    dk_out,
    dv_out,
    keys_s,
    values_s,
    q_s,
    do_s,
    norm_s,
    dot_s,
    starts_s,
    spans_s,
    key_win,
    value_win,
    key_t,
    ds_all,
    send_buf,
    recv_buf,
    join_buf,
    terms,
    stage_sem,
    in_sem,
    a2a_send,
    own_sem,
    kv_send,
    kv_recv,
    grad_send,
    grad_recv,
    join_recv,
    leap_send,
):
    scale = 1.0 / math.sqrt(HEAD_DIM)
    tok = lax.axis_index("tok")
    head = lax.axis_index("head")
    rows = QBLOCK // n_head
    half = QBLOCK // PIECES

    place = lax.rem(tok, ROW)
    ahead = ROW - place
    crosses = (ahead == REACH) & (tok + ahead < n_tok)

    def tok_at(step):
        return lax.rem(tok + (step + n_tok), n_tok)

    slot_rows = pl.ds(pl.multiple_of(head * rows, rows), rows)
    my_half = lax.div(head, n_head // PIECES)

    def columns(h):
        return pl.ds(pl.multiple_of(h * HEAD_DIM, HEAD_DIM), HEAD_DIM)

    barrier = pltpu.get_barrier_semaphore()
    with NS("xsig"):
        for step in range(1, n_head):
            pl.semaphore_signal(
                barrier, 1, device_id={"head": lax.rem(head + step, n_head)}, device_id_type=MESH
            )

        @pl.when(tok > 0)
        def _():
            pl.semaphore_signal(barrier, 1, device_id={"tok": tok_at(-1)}, device_id_type=MESH)

        if SPLIT:

            @pl.when((place == 0) & (tok > 0))
            def _():
                pl.semaphore_signal(
                    barrier, 1, device_id={"tok": tok_at(-REACH)}, device_id_type=MESH
                )


    sides = ((keys_hbm, keys_s, key_win), (values_hbm, values_s, value_win))
    with NS("xld"):
        stages = []
        for side, (source, stage, window) in enumerate(sides):
            pltpu.make_async_copy(
                source.at[:, columns(head)], window.at[0, slot_rows, :], own_sem.at[side, my_half]
            ).start()
            stages.append(pltpu.make_async_copy(source, stage, stage_sem.at[side]))
            stages[-1].start()
        loads = []
        for h in range(GROUP):
            block = pl.ds(h * QBLOCK, QBLOCK)
            cols = pl.ds(h * HEAD_DIM, HEAD_DIM)
            loads.append(
                pltpu.make_async_copy(query_hbm.at[:, cols], q_s.at[block, :], in_sem.at[h])
            )
            loads.append(
                pltpu.make_async_copy(
                    outgrad_hbm.at[:, cols], do_s.at[block, :], in_sem.at[GROUP + h]
                )
            )
        base = 2 * GROUP
        loads.append(pltpu.make_async_copy(norm_hbm, norm_s, in_sem.at[base]))
        loads.append(pltpu.make_async_copy(dot_hbm, dot_s, in_sem.at[base + 1]))
        loads.append(pltpu.make_async_copy(starts_hbm, starts_s, in_sem.at[base + 2]))
        loads.append(pltpu.make_async_copy(spans_hbm, spans_s, in_sem.at[base + 3]))
        for copy in loads:
            copy.start()
    with NS("xstage"):
        for copy in stages:
            copy.wait()
    with NS("xbar"):
        waits = n_head - 1 + jnp.where(tok + 1 < n_tok, 1, 0)
        if SPLIT:
            waits = waits + jnp.where(crosses, 1, 0)
        pl.semaphore_wait(barrier, waits)

    spreads = []
    with NS("xspread"):
        for side, (_, stage, window) in enumerate(sides):
            for step in range(1, n_head):
                peer = lax.rem(head + step, n_head)
                copy = pltpu.make_async_remote_copy(
                    src_ref=stage.at[:, columns(peer)],
                    dst_ref=window.at[0, slot_rows, :],
                    send_sem=a2a_send.at[side, step - 1],
                    recv_sem=own_sem.at[side, my_half],
                    device_id={"head": peer},
                    device_id_type=MESH,
                )
                copy.start()
                spreads.append(copy)

    def piece(slot, side, part):
        window = (key_win, value_win)[side]
        return window.at[slot, pl.ds(part * half, half), :]

    def forward(slot, side, part):
        return pltpu.make_async_remote_copy(
            src_ref=piece(slot, side, part),
            dst_ref=piece(slot + 1, side, part),
            send_sem=kv_send.at[slot, side, part],
            recv_sem=kv_recv.at[slot, side, part],
            device_id={"tok": tok_at(1)},
            device_id_type=MESH,
        )

    def leap(side, part):
        return pltpu.make_async_remote_copy(
            src_ref=piece(0, side, part),
            dst_ref=piece(REACH, side, part),
            send_sem=leap_send.at[side, part],
            recv_sem=kv_recv.at[REACH - 1, side, part],
            device_id={"tok": tok_at(REACH)},
            device_id_type=MESH,
        )

    def forwards(slot):
        if SPLIT and slot == REACH - 1:
            return (tok >= slot) & (place != ROW - 1)
        return (tok >= slot) & (tok + 1 < n_tok)

    pieces = [(side, part) for side in range(2) for part in range(PIECES)]
    for side, part in pieces:
        view = piece(0, side, part)
        with NS(f"xa2a{side}{part}"):
            pltpu.make_async_copy(view, view, own_sem.at[side, part]).wait()
        if SPLIT:

            @pl.when(crosses)
            def _():
                leap(side, part).start()

        @pl.when(forwards(0))
        def _():
            forward(0, side, part).start()

    with NS("xloads"):
        for copy in loads:
            copy.wait()

    start_row = starts_s[pl.ds(tok, 1), :]
    span = spans_s[tok]
    row_iota = lax.broadcasted_iota(jnp.int32, (QBLOCK, QBLOCK), 0)
    col_iota = lax.broadcasted_iota(jnp.int32, (QBLOCK, QBLOCK), 1)

    def block(slot):
        key = key_win[slot]
        value = value_win[slot]
        key_pos = row_iota + (tok - slot) * QBLOCK
        least = jnp.where(slot < span, start_row, FAR)
        allowed = key_pos >= least
        if slot == 0:
            allowed = allowed & (row_iota <= col_iota)
        value_term = jnp.zeros((QBLOCK, HEAD_DIM), jnp.float32)
        key_term = jnp.zeros((QBLOCK, HEAD_DIM), jnp.float32)
        for pair in range(GROUP // 2):
            block_rows = pl.ds(pair * 2 * QBLOCK, 2 * QBLOCK)
            q_pair = q_s[block_rows, :]
            do_pair = do_s[block_rows, :]
            scores = matmul(key, q_pair, NT)
            prob_grad = matmul(value, do_pair, NT)
            lows, grads = [], []
            for e in range(2):
                h = pair * 2 + e
                lanes = slice(e * QBLOCK, (e + 1) * QBLOCK)
                probs = jnp.where(
                    allowed, jnp.exp(scores[:, lanes] * scale - norm_s[pl.ds(h, 1), :]), 0.0
                )
                lows.append(probs.astype(jnp.bfloat16))
                grads.append(
                    (probs * (prob_grad[:, lanes] - dot_s[pl.ds(h, 1), :])).astype(jnp.bfloat16)
                )
            low = jnp.concatenate(lows, axis=1)
            grad = jnp.concatenate(grads, axis=1)
            ds_all[slot, :, block_rows] = grad
            value_term = value_term + matmul(low, do_pair, NN)
            key_term = key_term + matmul(grad, q_pair, NN)
        key_t[:, pl.ds(slot * QBLOCK, QBLOCK)] = key.T
        return key_term * scale, value_term

    def home(slot):
        return pltpu.make_async_remote_copy(
            src_ref=send_buf.at[slot - 1],
            dst_ref=recv_buf.at[slot - 1],
            send_sem=grad_send.at[slot - 1],
            recv_sem=grad_recv.at[slot - 1],
            device_id={"tok": tok_at(-slot)},
            device_id_type=MESH,
        )

    def onward(slot):
        return pltpu.make_async_remote_copy(
            src_ref=send_buf.at[slot - 1],
            dst_ref=join_buf.at[slot - 1],
            send_sem=grad_send.at[slot - 1],
            recv_sem=join_recv.at[slot - 1],
            device_id={"tok": tok_at(1)},
            device_id_type=MESH,
        )

    def goes_on(slot):
        if slot < JOIN or slot == REACH:
            return False
        return (place != ROW - 1) if SPLIT else (tok + 1 < n_tok)

    def joins(slot):
        if slot <= JOIN:
            return False
        return ((place != 0) if SPLIT else (tok > 0)) & (tok >= slot)

    def compute(slot):
        with NS(f"xblock{slot}"):
            both = block(slot)
            for side in range(2):
                terms[slot, side] = both[side]

    def ship(slot):
        with NS(f"xship{slot}"):
            if joins(slot) is False:
                for side in range(2):
                    send_buf[slot - 1, side] = terms[slot, side].astype(jnp.bfloat16)
            else:

                @pl.when(joins(slot))
                def _():
                    onward(slot - 1).wait_recv()
                    for side in range(2):
                        send_buf[slot - 1, side] = (
                            terms[slot, side] + join_buf[slot - 2, side].astype(jnp.float32)
                        ).astype(jnp.bfloat16)

                @pl.when(jnp.logical_not(joins(slot)))
                def _():
                    for side in range(2):
                        send_buf[slot - 1, side] = terms[slot, side].astype(jnp.bfloat16)

            passing = goes_on(slot)
            if passing is False:
                home(slot).start()
            else:

                @pl.when(passing)
                def _():
                    onward(slot).start()

                @pl.when(jnp.logical_not(passing))
                def _():
                    if SPLIT:
                        home(slot).start()

    def arrive(slot):
        for side, part in pieces:
            with NS(f"xkv{slot}{side}{part}"):
                forward(slot - 1, side, part).wait_recv()
            if slot < REACH:

                @pl.when(forwards(slot))
                def _():
                    forward(slot, side, part).start()

    compute(0)
    for slot in range(1, REACH + 1):

        @pl.when(tok >= slot)
        def _():
            arrive(slot)
            compute(slot)
            if slot < REACH:
                ship(slot)

        @pl.when(tok < slot)
        def _():
            ds_all[slot] = jnp.zeros((QBLOCK, GROUP * QBLOCK), jnp.bfloat16)
            key_t[:, pl.ds(slot * QBLOCK, QBLOCK)] = jnp.zeros((HEAD_DIM, QBLOCK), jnp.bfloat16)

    with NS("xdq"):
        for pair in range(GROUP // 2):
            lanes = pl.ds(pair * 2 * QBLOCK, 2 * QBLOCK)
            grad = ds_all[:, :, lanes].reshape((REACH + 1) * QBLOCK, 2 * QBLOCK)
            dq_t = matmul(key_t[...], grad, NN) * scale
            for e in range(2):
                h = pair * 2 + e
                dq_out[:, pl.ds(h * HEAD_DIM, HEAD_DIM)] = (
                    dq_t[:, e * QBLOCK : (e + 1) * QBLOCK].T.astype(jnp.bfloat16)
                )

    @pl.when(tok >= REACH)
    def _():
        ship(REACH)

    for slot in range(1, REACH + 1):
        expected = tok + slot < n_tok
        if JOIN <= slot < REACH:
            if not SPLIT:
                continue
            expected = place + slot == ROW - 1
        with NS(f"xgrad{slot}"):

            @pl.when(expected)
            def _():
                home(slot).wait_recv()
                for side in range(2):
                    terms[0, side] += recv_buf[slot - 1, side].astype(jnp.float32)

    for side, out in enumerate((dk_out, dv_out)):
        out[...] = terms[0, side].astype(jnp.bfloat16)
    with NS("xsends"):
        for copy in spreads:
            copy.wait_send()
        for side, part in pieces:
            if SPLIT:

                @pl.when(crosses)
                def _():
                    leap(side, part).wait_send()

        for slot in range(REACH):

            @pl.when(forwards(slot))
            def _():
                for side, part in pieces:
                    forward(slot, side, part).wait_send()

    with NS("xsendg"):
        for slot in range(1, REACH + 1):

            @pl.when(tok >= slot)
            def _():
                home(slot).wait_send()


def store(dq_ref, dk_ref, dv_ref, dq_hbm, dk_hbm, dv_hbm, sems):
    copies = [
        pltpu.make_async_copy(source, target, sems.at[index])
        for index, (source, target) in enumerate(
            ((dq_ref, dq_hbm), (dk_ref, dk_hbm), (dv_ref, dv_hbm))
        )
    ]
    for copy in copies:
        copy.start()
    for copy in copies:
        copy.wait()


def solution(mesh):
    n_tok = mesh.shape["tok"]
    n_head = mesh.shape["head"]
    slots = REACH + 1
    bf16, f32 = jnp.bfloat16, jnp.float32

    def per_device(query, keys, values, out_grad, log_norm, row_dot, doc_start, spans):
        starts = doc_start.reshape(n_tok, QBLOCK)
        anywhere = pl.BlockSpec(memory_space=pl.ANY)
        outside = pl.BlockSpec(memory_space=pltpu.HBM)
        inside = pl.BlockSpec(memory_space=pltpu.VMEM)
        shapes = (
            jax.ShapeDtypeStruct((QBLOCK, GROUP * HEAD_DIM), bf16),
            jax.ShapeDtypeStruct((QBLOCK, HEAD_DIM), bf16),
            jax.ShapeDtypeStruct((QBLOCK, HEAD_DIM), bf16),
        )
        grads = pl.pallas_call(
            functools.partial(kernel, n_tok, n_head),
            out_shape=tuple(pltpu.VMEM(shape.shape, shape.dtype) for shape in shapes),
            in_specs=[outside] * 8,
            out_specs=(inside,) * 3,
            scratch_shapes=[
                pltpu.VMEM((QBLOCK // n_head, KV_HEADS * HEAD_DIM), bf16),
                pltpu.VMEM((QBLOCK // n_head, KV_HEADS * HEAD_DIM), bf16),
                pltpu.VMEM((GROUP * QBLOCK, HEAD_DIM), bf16),
                pltpu.VMEM((GROUP * QBLOCK, HEAD_DIM), bf16),
                pltpu.VMEM((GROUP, QBLOCK), f32),
                pltpu.VMEM((GROUP, QBLOCK), f32),
                pltpu.VMEM((n_tok, QBLOCK), jnp.int32),
                pltpu.SMEM((n_tok,), jnp.int32),
                pltpu.VMEM((slots, QBLOCK, HEAD_DIM), bf16),
                pltpu.VMEM((slots, QBLOCK, HEAD_DIM), bf16),
                pltpu.VMEM((HEAD_DIM, slots * QBLOCK), bf16),
                pltpu.VMEM((slots, QBLOCK, GROUP * QBLOCK), bf16),
                pltpu.VMEM((REACH, 2, QBLOCK, HEAD_DIM), bf16),
                pltpu.VMEM((REACH, 2, QBLOCK, HEAD_DIM), bf16),
                pltpu.VMEM((REACH, 2, QBLOCK, HEAD_DIM), bf16),
                pltpu.VMEM((slots, 2, QBLOCK, HEAD_DIM), f32),
                pltpu.SemaphoreType.DMA((2,)),
                pltpu.SemaphoreType.DMA((2 * GROUP + 4,)),
                pltpu.SemaphoreType.DMA((2, n_head - 1)),
                pltpu.SemaphoreType.DMA((2, PIECES)),
                pltpu.SemaphoreType.DMA((REACH, 2, PIECES)),
                pltpu.SemaphoreType.DMA((REACH, 2, PIECES)),
                pltpu.SemaphoreType.DMA((REACH,)),
                pltpu.SemaphoreType.DMA((REACH,)),
                pltpu.SemaphoreType.DMA((REACH,)),
                pltpu.SemaphoreType.DMA((2, PIECES)),
            ],
            compiler_params=pltpu.CompilerParams(
                collective_id=0, has_side_effects=True
            ),
        )(query, keys, values, out_grad, log_norm, row_dot, starts, spans)
        return pl.pallas_call(
            store,
            out_shape=shapes,
            in_specs=[inside] * 3,
            out_specs=(anywhere,) * 3,
            scratch_shapes=[pltpu.SemaphoreType.DMA((3,))],
            compiler_params=pltpu.CompilerParams(vmem_limit_bytes=4 << 20),
        )(*grads)

    return jax.shard_map(
        per_device,
        mesh=mesh,
        in_specs=(
            P("tok", "head"),
            P(("tok", "head"), None),
            P(("tok", "head"), None),
            P("tok", "head"),
            P("head", "tok"),
            P("head", "tok"),
            P(),
            P(),
        ),
        out_specs=(P("tok", "head"), P("tok", "head"), P("tok", "head")),
        check_vma=False,
    )
```

time: 50.5 us -> 44.2 us (0.88)
  the two profiles are of different devices: /device:TPU:32 before, /device:TPU:24 now
where the time goes in v3:
time: 44.2 us; the launch traced here: 44 us
  Pallas kernels  43.3 us (98%)
  between operations  0.64 us (1%)
    pallas_call x1, Pallas kernels, per_device(): pl.pallas_call(functools.partial(kernel, n_tok, n_head), out_shape=tuple(...  42.6 us

profile of v3, /device:TPU:24, one launch (start us, length us, event | category | flops | bytes accessed | tf_op | source)
XLA Modules:
  0.0 44.0 jit_solution(1703399147785342368)
XLA Ops:
  0.6 42.6 %shard_map.103 = (bf16[128,1024]{1,0:T(8,128)(2,1)S(1)}, bf16[128,128]{1,0:T(8,128)(2,1)S(1)}, bf16[128,128]{1,0:T(8,128)(2,1)S(1)}) custom-call(bf16[128,1024]{1,0:T(8,128)(2,1)} %query_hbm.1, bf16[16,1024]{1,0:T(8,128)(2,1)} %keys_hbm.1, bf16[16,1024]{1,0:T(8,128)(2,1)} %values_hbm.1, bf16[128,1024]{1,0:T(8,128)(2,1)} %outgrad_hbm.1, f32[8,128]{1,0:T(8,128)} %norm_hbm.1, ...), custom_call_target="tpu_custom_call" | custom-call | tf_op jit(solution)/shard_map/pallas_call | solution.py:434
  43.2 0.7 %shard_map.104 = (bf16[128,1024]{1,0:T(8,128)(2,1)}, bf16[128,128]{1,0:T(8,128)(2,1)}, bf16[128,128]{1,0:T(8,128)(2,1)}) custom-call(bf16[128,1024]{1,0:T(8,128)(2,1)S(1)} %get-tuple-element.6.dq_ref, bf16[128,128]{1,0:T(8,128)(2,1)S(1)} %get-tuple-element.7.dk_ref, bf16[128,128]{1,0:T(8,128)(2,1)S(1)} %get-tuple-element.8.dv_ref), custom_call_target="tpu_custom_call" | custom-call | tf_op jit(solution)/shard_map/pallas_call | solution.py:471

commit v4 on v3

--- a/solution.py
+++ b/solution.py
@@ -14,13 +14,12 @@
 QBLOCK = 128
 REACH = 5
 GROUP = HEADS // KV_HEADS
-PIECES = 2
+PIECES = 4
 MESH = pl.DeviceIdType.MESH
 FAR = 1 << 30
 NS = jax.named_scope
 JOIN = 3
 ROW = 32
-SPLIT = True
 
 NT = (((1,), (1,)), ((), ()))
 NN = (((1,), (0,)), ((), ()))
@@ -69,7 +68,8 @@
     grad_send,
     grad_recv,
     join_recv,
-    leap_send,
+    next_send,
+    turn,
 ):
     scale = 1.0 / math.sqrt(HEAD_DIM)
     tok = lax.axis_index("tok")
@@ -78,8 +78,6 @@
     half = QBLOCK // PIECES
 
     place = lax.rem(tok, ROW)
-    ahead = ROW - place
-    crosses = (ahead == REACH) & (tok + ahead < n_tok)
 
     def tok_at(step):
         return lax.rem(tok + (step + n_tok), n_tok)
@@ -99,16 +97,13 @@
 
         @pl.when(tok > 0)
         def _():
-            pl.semaphore_signal(barrier, 1, device_id={"tok": tok_at(-1)}, device_id_type=MESH)
-
-        if SPLIT:
-
-            @pl.when((place == 0) & (tok > 0))
-            def _():
+            for step in range(n_head):
                 pl.semaphore_signal(
-                    barrier, 1, device_id={"tok": tok_at(-REACH)}, device_id_type=MESH
+                    barrier,
+                    1,
+                    device_id={"tok": tok_at(-1), "head": lax.rem(head + step, n_head)},
+                    device_id_type=MESH,
                 )
-
 
     sides = ((keys_hbm, keys_s, key_win), (values_hbm, values_s, value_win))
     with NS("xld"):
@@ -142,13 +137,30 @@
         for copy in stages:
             copy.wait()
     with NS("xbar"):
-        waits = n_head - 1 + jnp.where(tok + 1 < n_tok, 1, 0)
-        if SPLIT:
-            waits = waits + jnp.where(crosses, 1, 0)
+        waits = n_head - 1 + jnp.where(tok + 1 < n_tok, n_head, 0)
         pl.semaphore_wait(barrier, waits)
+
+    def to_next(side, step):
+        _, stage, window = sides[side]
+        peer = lax.rem(head + step, n_head)
+        return pltpu.make_async_remote_copy(
+            src_ref=stage.at[:, columns(peer)],
+            dst_ref=window.at[1, slot_rows, :],
+            send_sem=next_send.at[side, step],
+            recv_sem=kv_recv.at[0, side, my_half],
+            device_id={"tok": tok_at(1), "head": peer},
+            device_id_type=MESH,
+        )
 
     spreads = []
     with NS("xspread"):
+        for side, (_, stage, window) in enumerate(sides):
+
+            @pl.when(tok + 1 < n_tok)
+            def _():
+                for step in range(n_head):
+                    to_next(side, step).start()
+
         for side, (_, stage, window) in enumerate(sides):
             for step in range(1, n_head):
                 peer = lax.rem(head + step, n_head)
@@ -177,19 +189,7 @@
             device_id_type=MESH,
         )
 
-    def leap(side, part):
-        return pltpu.make_async_remote_copy(
-            src_ref=piece(0, side, part),
-            dst_ref=piece(REACH, side, part),
-            send_sem=leap_send.at[side, part],
-            recv_sem=kv_recv.at[REACH - 1, side, part],
-            device_id={"tok": tok_at(REACH)},
-            device_id_type=MESH,
-        )
-
     def forwards(slot):
-        if SPLIT and slot == REACH - 1:
-            return (tok >= slot) & (place != ROW - 1)
         return (tok >= slot) & (tok + 1 < n_tok)
 
     pieces = [(side, part) for side in range(2) for part in range(PIECES)]
@@ -197,15 +197,6 @@
         view = piece(0, side, part)
         with NS(f"xa2a{side}{part}"):
             pltpu.make_async_copy(view, view, own_sem.at[side, part]).wait()
-        if SPLIT:
-
-            @pl.when(crosses)
-            def _():
-                leap(side, part).start()
-
-        @pl.when(forwards(0))
-        def _():
-            forward(0, side, part).start()
 
     with NS("xloads"):
         for copy in loads:
@@ -274,12 +265,12 @@
     def goes_on(slot):
         if slot < JOIN or slot == REACH:
             return False
-        return (place != ROW - 1) if SPLIT else (tok + 1 < n_tok)
+        return place != ROW - 1
 
     def joins(slot):
         if slot <= JOIN:
             return False
-        return ((place != 0) if SPLIT else (tok > 0)) & (tok >= slot)
+        return (place != 0) & (tok >= slot)
 
     def compute(slot):
         with NS(f"xblock{slot}"):
@@ -318,13 +309,13 @@
 
                 @pl.when(jnp.logical_not(passing))
                 def _():
-                    if SPLIT:
-                        home(slot).start()
+                    home(slot).start()
 
     def arrive(slot):
         for side, part in pieces:
             with NS(f"xkv{slot}{side}{part}"):
-                forward(slot - 1, side, part).wait_recv()
+                view = piece(slot, side, part)
+                pltpu.make_async_copy(view, view, kv_recv.at[slot - 1, side, part]).wait()
             if slot < REACH:
 
                 @pl.when(forwards(slot))
@@ -345,6 +336,20 @@
         def _():
             ds_all[slot] = jnp.zeros((QBLOCK, GROUP * QBLOCK), jnp.bfloat16)
             key_t[:, pl.ds(slot * QBLOCK, QBLOCK)] = jnp.zeros((HEAD_DIM, QBLOCK), jnp.bfloat16)
+
+    early = (place == 0) & (tok >= REACH)
+
+    crossing = (place < REACH) & (tok >= ROW)
+
+    def pass_turn():
+        @pl.when(crossing & (place < REACH - 1))
+        def _():
+            pl.semaphore_signal(turn, 1, device_id={"tok": tok_at(1)}, device_id_type=MESH)
+
+    @pl.when(early)
+    def _():
+        ship(REACH)
+        pass_turn()
 
     with NS("xdq"):
         for pair in range(GROUP // 2):
@@ -357,15 +362,18 @@
                     dq_t[:, e * QBLOCK : (e + 1) * QBLOCK].T.astype(jnp.bfloat16)
                 )
 
-    @pl.when(tok >= REACH)
+    @pl.when((tok >= REACH) & jnp.logical_not(early))
     def _():
+        @pl.when(crossing)
+        def _():
+            pl.semaphore_wait(turn, 1)
+
         ship(REACH)
+        pass_turn()
 
     for slot in range(1, REACH + 1):
         expected = tok + slot < n_tok
         if JOIN <= slot < REACH:
-            if not SPLIT:
-                continue
             expected = place + slot == ROW - 1
         with NS(f"xgrad{slot}"):
 
@@ -380,14 +388,13 @@
     with NS("xsends"):
         for copy in spreads:
             copy.wait_send()
-        for side, part in pieces:
-            if SPLIT:
-
-                @pl.when(crosses)
-                def _():
-                    leap(side, part).wait_send()
-
-        for slot in range(REACH):
+        @pl.when(tok + 1 < n_tok)
+        def _():
+            for side in range(2):
+                for step in range(n_head):
+                    to_next(side, step).wait_send()
+
+        for slot in range(1, REACH):
 
             @pl.when(forwards(slot))
             def _():
@@ -462,7 +469,8 @@
                 pltpu.SemaphoreType.DMA((REACH,)),
                 pltpu.SemaphoreType.DMA((REACH,)),
                 pltpu.SemaphoreType.DMA((REACH,)),
-                pltpu.SemaphoreType.DMA((2, PIECES)),
+                pltpu.SemaphoreType.DMA((2, n_head)),
+                pltpu.SemaphoreType.REGULAR,
             ],
             compiler_params=pltpu.CompilerParams(
                 collective_id=0, has_side_effects=True

time: 44.2 us -> 43.1 us (0.975)
  the two profiles are of different devices: /device:TPU:24 before, /device:TPU:88 now
where the time goes in v4:
time: 43.1 us; the launch traced here: 42.9 us
  Pallas kernels  42.2 us (98%)
  between operations  0.64 us (1%)
    pallas_call x1, Pallas kernels, per_device(): pl.pallas_call(functools.partial(kernel, n_tok, n_head), out_shape=tuple(...  41.5 us

profile of v4, /device:TPU:88, one launch (start us, length us, event | category | flops | bytes accessed | tf_op | source)
XLA Modules:
  0.0 42.9 jit_solution(2570527360519175097)
XLA Ops:
  0.6 41.5 %shard_map.103 = (bf16[128,1024]{1,0:T(8,128)(2,1)S(1)}, bf16[128,128]{1,0:T(8,128)(2,1)S(1)}, bf16[128,128]{1,0:T(8,128)(2,1)S(1)}) custom-call(bf16[128,1024]{1,0:T(8,128)(2,1)} %query_hbm.1, bf16[16,1024]{1,0:T(8,128)(2,1)} %keys_hbm.1, bf16[16,1024]{1,0:T(8,128)(2,1)} %values_hbm.1, bf16[128,1024]{1,0:T(8,128)(2,1)} %outgrad_hbm.1, f32[8,128]{1,0:T(8,128)} %norm_hbm.1, ...), custom_call_target="tpu_custom_call" | custom-call | tf_op jit(solution)/shard_map/pallas_call | solution.py:441
  42.1 0.7 %shard_map.104 = (bf16[128,1024]{1,0:T(8,128)(2,1)}, bf16[128,128]{1,0:T(8,128)(2,1)}, bf16[128,128]{1,0:T(8,128)(2,1)}) custom-call(bf16[128,1024]{1,0:T(8,128)(2,1)S(1)} %get-tuple-element.6.dq_ref, bf16[128,128]{1,0:T(8,128)(2,1)S(1)} %get-tuple-element.7.dk_ref, bf16[128,128]{1,0:T(8,128)(2,1)S(1)} %get-tuple-element.8.dv_ref), custom_call_target="tpu_custom_call" | custom-call | tf_op jit(solution)/shard_map/pallas_call | solution.py:479

commit v5 on v4

--- a/solution.py
+++ b/solution.py
@@ -43,18 +43,16 @@
     dq_out,
     dk_out,
     dv_out,
-    keys_s,
-    values_s,
-    q_s,
-    do_s,
-    norm_s,
-    dot_s,
+    stage_s,
+    rows_s,
+    norms_s,
     starts_s,
     spans_s,
     key_win,
     value_win,
     key_t,
     ds_all,
+    probs_s,
     send_buf,
     recv_buf,
     join_buf,
@@ -105,37 +103,30 @@
                     device_id_type=MESH,
                 )
 
-    sides = ((keys_hbm, keys_s, key_win), (values_hbm, values_s, value_win))
+    sides = ((keys_hbm, stage_s.at[0], key_win), (values_hbm, stage_s.at[1], value_win))
+    q_s, do_s = rows_s.at[0], rows_s.at[1]
+    norm_s, dot_s = norms_s.at[0], norms_s.at[1]
     with NS("xld"):
-        stages = []
         for side, (source, stage, window) in enumerate(sides):
             pltpu.make_async_copy(
-                source.at[:, columns(head)], window.at[0, slot_rows, :], own_sem.at[side, my_half]
+                source.at[:, columns(head)], window.at[0, slot_rows, :], own_sem.at[side]
             ).start()
-            stages.append(pltpu.make_async_copy(source, stage, stage_sem.at[side]))
-            stages[-1].start()
-        loads = []
+            pltpu.make_async_copy(source, stage, stage_sem).start()
         for h in range(GROUP):
             block = pl.ds(h * QBLOCK, QBLOCK)
             cols = pl.ds(h * HEAD_DIM, HEAD_DIM)
-            loads.append(
-                pltpu.make_async_copy(query_hbm.at[:, cols], q_s.at[block, :], in_sem.at[h])
-            )
-            loads.append(
-                pltpu.make_async_copy(
-                    outgrad_hbm.at[:, cols], do_s.at[block, :], in_sem.at[GROUP + h]
-                )
-            )
-        base = 2 * GROUP
-        loads.append(pltpu.make_async_copy(norm_hbm, norm_s, in_sem.at[base]))
-        loads.append(pltpu.make_async_copy(dot_hbm, dot_s, in_sem.at[base + 1]))
-        loads.append(pltpu.make_async_copy(starts_hbm, starts_s, in_sem.at[base + 2]))
-        loads.append(pltpu.make_async_copy(spans_hbm, spans_s, in_sem.at[base + 3]))
-        for copy in loads:
-            copy.start()
+            pltpu.make_async_copy(query_hbm.at[:, cols], q_s.at[block, :], in_sem.at[0]).start()
+            pltpu.make_async_copy(outgrad_hbm.at[:, cols], do_s.at[block, :], in_sem.at[0]).start()
+        pltpu.make_async_copy(norm_hbm, norm_s, in_sem.at[1]).start()
+        pltpu.make_async_copy(dot_hbm, dot_s, in_sem.at[1]).start()
+        pltpu.make_async_copy(starts_hbm, starts_s, in_sem.at[2]).start()
+        pltpu.make_async_copy(spans_hbm, spans_s, in_sem.at[3]).start()
+
+    def finished(view, sem):
+        pltpu.make_async_copy(view, view, sem).wait()
+
     with NS("xstage"):
-        for copy in stages:
-            copy.wait()
+        finished(stage_s, stage_sem)
     with NS("xbar"):
         waits = n_head - 1 + jnp.where(tok + 1 < n_tok, n_head, 0)
         pl.semaphore_wait(barrier, waits)
@@ -146,13 +137,12 @@
         return pltpu.make_async_remote_copy(
             src_ref=stage.at[:, columns(peer)],
             dst_ref=window.at[1, slot_rows, :],
-            send_sem=next_send.at[side, step],
-            recv_sem=kv_recv.at[0, side, my_half],
+            send_sem=next_send,
+            recv_sem=kv_recv.at[side * PIECES + my_half],
             device_id={"tok": tok_at(1), "head": peer},
             device_id_type=MESH,
         )
 
-    spreads = []
     with NS("xspread"):
         for side, (_, stage, window) in enumerate(sides):
 
@@ -164,27 +154,29 @@
         for side, (_, stage, window) in enumerate(sides):
             for step in range(1, n_head):
                 peer = lax.rem(head + step, n_head)
-                copy = pltpu.make_async_remote_copy(
+                pltpu.make_async_remote_copy(
                     src_ref=stage.at[:, columns(peer)],
                     dst_ref=window.at[0, slot_rows, :],
-                    send_sem=a2a_send.at[side, step - 1],
-                    recv_sem=own_sem.at[side, my_half],
+                    send_sem=a2a_send,
+                    recv_sem=own_sem.at[side],
                     device_id={"head": peer},
                     device_id_type=MESH,
-                )
-                copy.start()
-                spreads.append(copy)
+                ).start()
 
     def piece(slot, side, part):
         window = (key_win, value_win)[side]
         return window.at[slot, pl.ds(part * half, half), :]
+
+    def arrival(slot, side, part):
+        index = (slot - 1) * 2 * PIECES
+        return kv_recv.at[index + (side if slot == REACH else side * PIECES + part)]
 
     def forward(slot, side, part):
         return pltpu.make_async_remote_copy(
             src_ref=piece(slot, side, part),
             dst_ref=piece(slot + 1, side, part),
-            send_sem=kv_send.at[slot, side, part],
-            recv_sem=kv_recv.at[slot, side, part],
+            send_sem=kv_send.at[slot - 1],
+            recv_sem=arrival(slot + 1, side, part),
             device_id={"tok": tok_at(1)},
             device_id_type=MESH,
         )
@@ -193,54 +185,87 @@
         return (tok >= slot) & (tok + 1 < n_tok)
 
     pieces = [(side, part) for side in range(2) for part in range(PIECES)]
-    for side, part in pieces:
-        view = piece(0, side, part)
-        with NS(f"xa2a{side}{part}"):
-            pltpu.make_async_copy(view, view, own_sem.at[side, part]).wait()
-
+    with NS("xa2a"):
+        for side in range(2):
+            finished(sides[side][2].at[0], own_sem.at[side])
     with NS("xloads"):
-        for copy in loads:
-            copy.wait()
+        finished(rows_s, in_sem.at[0])
+        finished(norms_s, in_sem.at[1])
+        finished(starts_s, in_sem.at[2])
+        finished(spans_s, in_sem.at[3])
 
     start_row = starts_s[pl.ds(tok, 1), :]
     span = spans_s[tok]
     row_iota = lax.broadcasted_iota(jnp.int32, (QBLOCK, QBLOCK), 0)
     col_iota = lax.broadcasted_iota(jnp.int32, (QBLOCK, QBLOCK), 1)
 
+    def mask(slot):
+        key_pos = row_iota + (tok - slot) * QBLOCK
+        allowed = key_pos >= jnp.where(slot < span, start_row, FAR)
+        if slot == 0:
+            allowed = allowed & (row_iota <= col_iota)
+        return allowed
+
+    def pair_probs(key, pair, allowed):
+        scores = matmul(key, q_s[pl.ds(pair * 2 * QBLOCK, 2 * QBLOCK), :], NT)
+        probs = []
+        for e in range(2):
+            part = scores[:, e * QBLOCK : (e + 1) * QBLOCK] * scale
+            part = jnp.exp(part - norm_s[pl.ds(pair * 2 + e, 1), :])
+            probs.append(jnp.where(allowed, part, 0.0))
+        return probs
+
+    def pair_grads(value, pair, probs):
+        prob_grad = matmul(value, do_s[pl.ds(pair * 2 * QBLOCK, 2 * QBLOCK), :], NT)
+        grads = []
+        for e in range(2):
+            part = prob_grad[:, e * QBLOCK : (e + 1) * QBLOCK]
+            part = probs[e] * (part - dot_s[pl.ds(pair * 2 + e, 1), :])
+            grads.append(part.astype(jnp.bfloat16))
+        return jnp.concatenate(grads, axis=1)
+
+    def lowered(probs):
+        return jnp.concatenate([part.astype(jnp.bfloat16) for part in probs], axis=1)
+
     def block(slot):
         key = key_win[slot]
         value = value_win[slot]
-        key_pos = row_iota + (tok - slot) * QBLOCK
-        least = jnp.where(slot < span, start_row, FAR)
-        allowed = key_pos >= least
-        if slot == 0:
-            allowed = allowed & (row_iota <= col_iota)
+        allowed = mask(slot)
         value_term = jnp.zeros((QBLOCK, HEAD_DIM), jnp.float32)
         key_term = jnp.zeros((QBLOCK, HEAD_DIM), jnp.float32)
         for pair in range(GROUP // 2):
-            block_rows = pl.ds(pair * 2 * QBLOCK, 2 * QBLOCK)
-            q_pair = q_s[block_rows, :]
-            do_pair = do_s[block_rows, :]
-            scores = matmul(key, q_pair, NT)
-            prob_grad = matmul(value, do_pair, NT)
-            lows, grads = [], []
-            for e in range(2):
-                h = pair * 2 + e
-                lanes = slice(e * QBLOCK, (e + 1) * QBLOCK)
-                probs = jnp.where(
-                    allowed, jnp.exp(scores[:, lanes] * scale - norm_s[pl.ds(h, 1), :]), 0.0
-                )
-                lows.append(probs.astype(jnp.bfloat16))
-                grads.append(
-                    (probs * (prob_grad[:, lanes] - dot_s[pl.ds(h, 1), :])).astype(jnp.bfloat16)
-                )
-            low = jnp.concatenate(lows, axis=1)
-            grad = jnp.concatenate(grads, axis=1)
-            ds_all[slot, :, block_rows] = grad
-            value_term = value_term + matmul(low, do_pair, NN)
-            key_term = key_term + matmul(grad, q_pair, NN)
+            rows_of = pl.ds(pair * 2 * QBLOCK, 2 * QBLOCK)
+            probs = pair_probs(key, pair, allowed)
+            grad = pair_grads(value, pair, probs)
+            ds_all[slot, :, rows_of] = grad
+            value_term = value_term + matmul(lowered(probs), do_s[rows_of, :], NN)
+            key_term = key_term + matmul(grad, q_s[rows_of, :], NN)
         key_t[:, pl.ds(slot * QBLOCK, QBLOCK)] = key.T
         return key_term * scale, value_term
+
+    def value_half(slot):
+        key = key_win[slot]
+        allowed = mask(slot)
+        value_term = jnp.zeros((QBLOCK, HEAD_DIM), jnp.float32)
+        for pair in range(GROUP // 2):
+            rows_of = pl.ds(pair * 2 * QBLOCK, 2 * QBLOCK)
+            probs = pair_probs(key, pair, allowed)
+            for e in range(2):
+                probs_s[:, pl.ds((pair * 2 + e) * QBLOCK, QBLOCK)] = probs[e]
+            value_term = value_term + matmul(lowered(probs), do_s[rows_of, :], NN)
+        key_t[:, pl.ds(slot * QBLOCK, QBLOCK)] = key.T
+        terms[slot, 1] = value_term
+
+    def key_half(slot):
+        value = value_win[slot]
+        key_term = jnp.zeros((QBLOCK, HEAD_DIM), jnp.float32)
+        for pair in range(GROUP // 2):
+            rows_of = pl.ds(pair * 2 * QBLOCK, 2 * QBLOCK)
+            probs = [probs_s[:, pl.ds((pair * 2 + e) * QBLOCK, QBLOCK)] for e in range(2)]
+            grad = pair_grads(value, pair, probs)
+            ds_all[slot, :, rows_of] = grad
+            key_term = key_term + matmul(grad, q_s[rows_of, :], NN)
+        terms[slot, 0] = key_term * scale
 
     def home(slot):
         return pltpu.make_async_remote_copy(
@@ -257,7 +282,7 @@
             src_ref=send_buf.at[slot - 1],
             dst_ref=join_buf.at[slot - 1],
             send_sem=grad_send.at[slot - 1],
-            recv_sem=join_recv.at[slot - 1],
+            recv_sem=join_recv.at[slot - JOIN],
             device_id={"tok": tok_at(1)},
             device_id_type=MESH,
         )
@@ -311,25 +336,55 @@
                 def _():
                     home(slot).start()
 
+    def home_side(side):
+        return pltpu.make_async_remote_copy(
+            src_ref=send_buf.at[REACH - 1, side],
+            dst_ref=recv_buf.at[REACH - 1, side],
+            send_sem=grad_send.at[REACH - 1],
+            recv_sem=grad_recv.at[REACH - 1],
+            device_id={"tok": tok_at(-REACH)},
+            device_id_type=MESH,
+        )
+
+    early = (place == 0) & (tok >= REACH)
+
+    def early_side(side):
+        @pl.when(early)
+        def _():
+            send_buf[REACH - 1, side] = terms[REACH, side].astype(jnp.bfloat16)
+            home_side(side).start()
+
     def arrive(slot):
         for side, part in pieces:
             with NS(f"xkv{slot}{side}{part}"):
-                view = piece(slot, side, part)
-                pltpu.make_async_copy(view, view, kv_recv.at[slot - 1, side, part]).wait()
-            if slot < REACH:
-
-                @pl.when(forwards(slot))
-                def _():
-                    forward(slot, side, part).start()
+                finished(piece(slot, side, part), arrival(slot, side, part))
+
+            @pl.when(forwards(slot))
+            def _():
+                forward(slot, side, part).start()
+
+    def last():
+        with NS("xkv500"):
+            finished(key_win.at[REACH], arrival(REACH, 0, 0))
+        with NS("xhalf"):
+            value_half(REACH)
+        early_side(1)
+        with NS("xkv510"):
+            finished(value_win.at[REACH], arrival(REACH, 1, 0))
+        with NS("xblock5"):
+            key_half(REACH)
+        early_side(0)
 
     compute(0)
     for slot in range(1, REACH + 1):
 
         @pl.when(tok >= slot)
         def _():
-            arrive(slot)
-            compute(slot)
-            if slot < REACH:
+            if slot == REACH:
+                last()
+            else:
+                arrive(slot)
+                compute(slot)
                 ship(slot)
 
         @pl.when(tok < slot)
@@ -337,8 +392,6 @@
             ds_all[slot] = jnp.zeros((QBLOCK, GROUP * QBLOCK), jnp.bfloat16)
             key_t[:, pl.ds(slot * QBLOCK, QBLOCK)] = jnp.zeros((HEAD_DIM, QBLOCK), jnp.bfloat16)
 
-    early = (place == 0) & (tok >= REACH)
-
     crossing = (place < REACH) & (tok >= ROW)
 
     def pass_turn():
@@ -348,7 +401,6 @@
 
     @pl.when(early)
     def _():
-        ship(REACH)
         pass_turn()
 
     with NS("xdq"):
@@ -386,20 +438,17 @@
     for side, out in enumerate((dk_out, dv_out)):
         out[...] = terms[0, side].astype(jnp.bfloat16)
     with NS("xsends"):
-        for copy in spreads:
-            copy.wait_send()
+        finished(q_s.at[pl.ds(0, 2 * (n_head - 1) * rows), :], a2a_send)
+
         @pl.when(tok + 1 < n_tok)
         def _():
-            for side in range(2):
-                for step in range(n_head):
-                    to_next(side, step).wait_send()
+            finished(q_s.at[pl.ds(0, 2 * n_head * rows), :], next_send)
 
         for slot in range(1, REACH):
 
             @pl.when(forwards(slot))
             def _():
-                for side, part in pieces:
-                    forward(slot, side, part).wait_send()
+                finished(q_s.at[pl.ds(0, 2 * QBLOCK), :], kv_send.at[slot - 1])
 
     with NS("xsendg"):
         for slot in range(1, REACH + 1):
@@ -444,32 +493,30 @@
             in_specs=[outside] * 8,
             out_specs=(inside,) * 3,
             scratch_shapes=[
-                pltpu.VMEM((QBLOCK // n_head, KV_HEADS * HEAD_DIM), bf16),
-                pltpu.VMEM((QBLOCK // n_head, KV_HEADS * HEAD_DIM), bf16),
-                pltpu.VMEM((GROUP * QBLOCK, HEAD_DIM), bf16),
-                pltpu.VMEM((GROUP * QBLOCK, HEAD_DIM), bf16),
-                pltpu.VMEM((GROUP, QBLOCK), f32),
-                pltpu.VMEM((GROUP, QBLOCK), f32),
+                pltpu.VMEM((2, QBLOCK // n_head, KV_HEADS * HEAD_DIM), bf16),
+                pltpu.VMEM((2, GROUP * QBLOCK, HEAD_DIM), bf16),
+                pltpu.VMEM((2, GROUP, QBLOCK), f32),
                 pltpu.VMEM((n_tok, QBLOCK), jnp.int32),
                 pltpu.SMEM((n_tok,), jnp.int32),
                 pltpu.VMEM((slots, QBLOCK, HEAD_DIM), bf16),
                 pltpu.VMEM((slots, QBLOCK, HEAD_DIM), bf16),
                 pltpu.VMEM((HEAD_DIM, slots * QBLOCK), bf16),
                 pltpu.VMEM((slots, QBLOCK, GROUP * QBLOCK), bf16),
+                pltpu.VMEM((QBLOCK, GROUP * QBLOCK), f32),
                 pltpu.VMEM((REACH, 2, QBLOCK, HEAD_DIM), bf16),
                 pltpu.VMEM((REACH, 2, QBLOCK, HEAD_DIM), bf16),
                 pltpu.VMEM((REACH, 2, QBLOCK, HEAD_DIM), bf16),
                 pltpu.VMEM((slots, 2, QBLOCK, HEAD_DIM), f32),
+                pltpu.SemaphoreType.DMA(()),
+                pltpu.SemaphoreType.DMA((4,)),
+                pltpu.SemaphoreType.DMA(()),
                 pltpu.SemaphoreType.DMA((2,)),
-                pltpu.SemaphoreType.DMA((2 * GROUP + 4,)),
-                pltpu.SemaphoreType.DMA((2, n_head - 1)),
-                pltpu.SemaphoreType.DMA((2, PIECES)),
-                pltpu.SemaphoreType.DMA((REACH, 2, PIECES)),
-                pltpu.SemaphoreType.DMA((REACH, 2, PIECES)),
+                pltpu.SemaphoreType.DMA((REACH - 1,)),
+                pltpu.SemaphoreType.DMA(((REACH - 1) * 2 * PIECES + 2,)),
                 pltpu.SemaphoreType.DMA((REACH,)),
                 pltpu.SemaphoreType.DMA((REACH,)),
-                pltpu.SemaphoreType.DMA((REACH,)),
-                pltpu.SemaphoreType.DMA((2, n_head)),
+                pltpu.SemaphoreType.DMA((REACH - JOIN,)),
+                pltpu.SemaphoreType.DMA(()),
                 pltpu.SemaphoreType.REGULAR,
             ],
             compiler_params=pltpu.CompilerParams(

time: 43.1 us -> 42 us (0.974)
  Pallas kernels: 42.2 us -> 41.2 us
    pallas_call x1, Pallas kernels: 41.5 us -> 40.4 us  [per_device(): pl.pallas_call(functools.partial(kernel, n_tok, n_head), out_shape=tuple(...]
where the time goes in v5:
time: 42 us; the launch traced here: 41.8 us
  Pallas kernels  41.2 us (98%)
  between operations  0.64 us (2%)
    pallas_call x1, Pallas kernels, per_device(): pl.pallas_call(functools.partial(kernel, n_tok, n_head), out_shape=tuple(...  40.4 us

profile of v5, /device:TPU:88, one launch (start us, length us, event | category | flops | bytes accessed | tf_op | source)
XLA Modules:
  0.0 41.8 jit_solution(7901790624218374437)
XLA Ops:
  0.6 40.4 %shard_map.103 = (bf16[128,1024]{1,0:T(8,128)(2,1)S(1)}, bf16[128,128]{1,0:T(8,128)(2,1)S(1)}, bf16[128,128]{1,0:T(8,128)(2,1)S(1)}) custom-call(bf16[128,1024]{1,0:T(8,128)(2,1)} %query_hbm.1, bf16[16,1024]{1,0:T(8,128)(2,1)} %keys_hbm.1, bf16[16,1024]{1,0:T(8,128)(2,1)} %values_hbm.1, bf16[128,1024]{1,0:T(8,128)(2,1)} %outgrad_hbm.1, f32[8,128]{1,0:T(8,128)} %norm_hbm.1, ...), custom_call_target="tpu_custom_call" | custom-call | tf_op jit(solution)/shard_map/pallas_call | solution.py:490
  41.1 0.7 %shard_map.104 = (bf16[128,1024]{1,0:T(8,128)(2,1)}, bf16[128,128]{1,0:T(8,128)(2,1)}, bf16[128,128]{1,0:T(8,128)(2,1)}) custom-call(bf16[128,1024]{1,0:T(8,128)(2,1)S(1)} %get-tuple-element.6.dq_ref, bf16[128,128]{1,0:T(8,128)(2,1)S(1)} %get-tuple-element.7.dk_ref, bf16[128,128]{1,0:T(8,128)(2,1)S(1)} %get-tuple-element.8.dv_ref), custom_call_target="tpu_custom_call" | custom-call | tf_op jit(solution)/shard_map/pallas_call | solution.py:526

commit v6 on v5

--- a/solution.py
+++ b/solution.py
@@ -15,10 +15,11 @@
 REACH = 5
 GROUP = HEADS // KV_HEADS
 PIECES = 4
+STRIPS = 4
 MESH = pl.DeviceIdType.MESH
 FAR = 1 << 30
 NS = jax.named_scope
-JOIN = 3
+JOIN = 4
 ROW = 32
 
 NT = (((1,), (1,)), ((), ()))
@@ -348,11 +349,20 @@
 
     early = (place == 0) & (tok >= REACH)
 
+    crossing = (place < REACH) & (tok >= ROW)
+
+    def pass_turn():
+        @pl.when(crossing & (place < REACH - 1))
+        def _():
+            pl.semaphore_signal(turn, 1, device_id={"tok": tok_at(1)}, device_id_type=MESH)
+
     def early_side(side):
         @pl.when(early)
         def _():
             send_buf[REACH - 1, side] = terms[REACH, side].astype(jnp.bfloat16)
             home_side(side).start()
+            if side == 1:
+                pass_turn()
 
     def arrive(slot):
         for side, part in pieces:
@@ -392,17 +402,6 @@
             ds_all[slot] = jnp.zeros((QBLOCK, GROUP * QBLOCK), jnp.bfloat16)
             key_t[:, pl.ds(slot * QBLOCK, QBLOCK)] = jnp.zeros((HEAD_DIM, QBLOCK), jnp.bfloat16)
 
-    crossing = (place < REACH) & (tok >= ROW)
-
-    def pass_turn():
-        @pl.when(crossing & (place < REACH - 1))
-        def _():
-            pl.semaphore_signal(turn, 1, device_id={"tok": tok_at(1)}, device_id_type=MESH)
-
-    @pl.when(early)
-    def _():
-        pass_turn()
-
     with NS("xdq"):
         for pair in range(GROUP // 2):
             lanes = pl.ds(pair * 2 * QBLOCK, 2 * QBLOCK)
@@ -459,11 +458,14 @@
 
 
 def store(dq_ref, dk_ref, dv_ref, dq_hbm, dk_hbm, dv_hbm, sems):
+    part = QBLOCK // STRIPS
+    moves = [
+        (dq_ref.at[pl.ds(strip * part, part), :], dq_hbm.at[pl.ds(strip * part, part), :])
+        for strip in range(STRIPS)
+    ] + [(dk_ref, dk_hbm), (dv_ref, dv_hbm)]
     copies = [
         pltpu.make_async_copy(source, target, sems.at[index])
-        for index, (source, target) in enumerate(
-            ((dq_ref, dq_hbm), (dk_ref, dk_hbm), (dv_ref, dv_hbm))
-        )
+        for index, (source, target) in enumerate(moves)
     ]
     for copy in copies:
         copy.start()
@@ -528,7 +530,7 @@
             out_shape=shapes,
             in_specs=[inside] * 3,
             out_specs=(anywhere,) * 3,
-            scratch_shapes=[pltpu.SemaphoreType.DMA((3,))],
+            scratch_shapes=[pltpu.SemaphoreType.DMA((STRIPS + 2,))],
             compiler_params=pltpu.CompilerParams(vmem_limit_bytes=4 << 20),
         )(*grads)
 

time: 42 us -> 41.2 us (0.981)
  the two profiles are of different devices: /device:TPU:88 before, /device:TPU:24 now
where the time goes in v6:
time: 41.2 us; the launch traced here: 41 us
  Pallas kernels  40.4 us (98%)
  between operations  0.64 us (2%)
    pallas_call x1, Pallas kernels, per_device(): pl.pallas_call(functools.partial(kernel, n_tok, n_head), out_shape=tuple(...  39.6 us

profile of v6, /device:TPU:24, one launch (start us, length us, event | category | flops | bytes accessed | tf_op | source)
XLA Modules:
  0.0 41.0 jit_solution(15761852790186851655)
XLA Ops:
  0.6 39.6 %shard_map.103 = (bf16[128,1024]{1,0:T(8,128)(2,1)S(1)}, bf16[128,128]{1,0:T(8,128)(2,1)S(1)}, bf16[128,128]{1,0:T(8,128)(2,1)S(1)}) custom-call(bf16[128,1024]{1,0:T(8,128)(2,1)} %query_hbm.1, bf16[16,1024]{1,0:T(8,128)(2,1)} %keys_hbm.1, bf16[16,1024]{1,0:T(8,128)(2,1)} %values_hbm.1, bf16[128,1024]{1,0:T(8,128)(2,1)} %outgrad_hbm.1, f32[8,128]{1,0:T(8,128)} %norm_hbm.1, ...), custom_call_target="tpu_custom_call" | custom-call | tf_op jit(solution)/shard_map/pallas_call | solution.py:492
  40.2 0.8 %shard_map.104 = (bf16[128,1024]{1,0:T(8,128)(2,1)}, bf16[128,128]{1,0:T(8,128)(2,1)}, bf16[128,128]{1,0:T(8,128)(2,1)}) custom-call(bf16[128,1024]{1,0:T(8,128)(2,1)S(1)} %get-tuple-element.6.dq_ref, bf16[128,128]{1,0:T(8,128)(2,1)S(1)} %get-tuple-element.7.dk_ref, bf16[128,128]{1,0:T(8,128)(2,1)S(1)} %get-tuple-element.8.dv_ref), custom_call_target="tpu_custom_call" | custom-call | tf_op jit(solution)/shard_map/pallas_call | solution.py:528

commit v7 on v6

--- a/solution.py
+++ b/solution.py
@@ -144,16 +144,18 @@
             device_id_type=MESH,
         )
 
+    order = sorted(range(n_head), key=lambda step: abs(step - n_head // 2))
+    order.sort(key=lambda step: step == 0)
     with NS("xspread"):
         for side, (_, stage, window) in enumerate(sides):
 
             @pl.when(tok + 1 < n_tok)
             def _():
-                for step in range(n_head):
+                for step in order:
                     to_next(side, step).start()
 
         for side, (_, stage, window) in enumerate(sides):
-            for step in range(1, n_head):
+            for step in order[:-1]:
                 peer = lax.rem(head + step, n_head)
                 pltpu.make_async_remote_copy(
                     src_ref=stage.at[:, columns(peer)],
@@ -186,9 +188,6 @@
         return (tok >= slot) & (tok + 1 < n_tok)
 
     pieces = [(side, part) for side in range(2) for part in range(PIECES)]
-    with NS("xa2a"):
-        for side in range(2):
-            finished(sides[side][2].at[0], own_sem.at[side])
     with NS("xloads"):
         finished(rows_s, in_sem.at[0])
         finished(norms_s, in_sem.at[1])
@@ -385,7 +384,16 @@
             key_half(REACH)
         early_side(0)
 
-    compute(0)
+    def first():
+        with NS("xa2a"):
+            for side in range(2):
+                finished(sides[side][2].at[0], own_sem.at[side])
+        compute(0)
+
+    @pl.when(place == 0)
+    def _():
+        first()
+
     for slot in range(1, REACH + 1):
 
         @pl.when(tok >= slot)
@@ -394,6 +402,12 @@
                 last()
             else:
                 arrive(slot)
+                if slot == 1:
+
+                    @pl.when(place != 0)
+                    def _():
+                        first()
+
                 compute(slot)
                 ship(slot)
 

time: 41.2 us -> 40.9 us (level)
  Pallas kernels: 40.4 us -> 39.8 us
    pallas_call x1, Pallas kernels: 39.6 us -> 39 us  [per_device(): pl.pallas_call(functools.partial(kernel, n_tok, n_head), out_shape=tuple(...]
where the time goes in v7:
time: 40.9 us; the launch traced here: 40.4 us
  Pallas kernels  39.8 us (97%)
  between operations  0.64 us (2%)
    pallas_call x1, Pallas kernels, per_device(): pl.pallas_call(functools.partial(kernel, n_tok, n_head), out_shape=tuple(...  39 us

profile of v7, /device:TPU:24, one launch (start us, length us, event | category | flops | bytes accessed | tf_op | source)
XLA Modules:
  0.0 40.4 jit_solution(5033347022075199298)
XLA Ops:
  0.6 39.0 %shard_map.103 = (bf16[128,1024]{1,0:T(8,128)(2,1)S(1)}, bf16[128,128]{1,0:T(8,128)(2,1)S(1)}, bf16[128,128]{1,0:T(8,128)(2,1)S(1)}) custom-call(bf16[128,1024]{1,0:T(8,128)(2,1)} %query_hbm.1, bf16[16,1024]{1,0:T(8,128)(2,1)} %keys_hbm.1, bf16[16,1024]{1,0:T(8,128)(2,1)} %values_hbm.1, bf16[128,1024]{1,0:T(8,128)(2,1)} %outgrad_hbm.1, f32[8,128]{1,0:T(8,128)} %norm_hbm.1, ...), custom_call_target="tpu_custom_call" | custom-call | tf_op jit(solution)/shard_map/pallas_call | solution.py:506
  39.7 0.8 %shard_map.104 = (bf16[128,1024]{1,0:T(8,128)(2,1)}, bf16[128,128]{1,0:T(8,128)(2,1)}, bf16[128,128]{1,0:T(8,128)(2,1)}) custom-call(bf16[128,1024]{1,0:T(8,128)(2,1)S(1)} %get-tuple-element.6.dq_ref, bf16[128,128]{1,0:T(8,128)(2,1)S(1)} %get-tuple-element.7.dk_ref, bf16[128,128]{1,0:T(8,128)(2,1)S(1)} %get-tuple-element.8.dv_ref), custom_call_target="tpu_custom_call" | custom-call | tf_op jit(solution)/shard_map/pallas_call | solution.py:542

commit v8 on v7

--- a/solution.py
+++ b/solution.py
@@ -433,8 +433,8 @@
         def _():
             pl.semaphore_wait(turn, 1)
 
+        pass_turn()
         ship(REACH)
-        pass_turn()
 
     for slot in range(1, REACH + 1):
         expected = tok + slot < n_tok

time: 40.9 us -> 40.7 us (level)
  no operation moved by 1% of the time
where the time goes in v8:
time: 40.7 us; the launch traced here: 40.4 us
  Pallas kernels  39.8 us (98%)
  between operations  0.64 us (2%)
    pallas_call x1, Pallas kernels, per_device(): pl.pallas_call(functools.partial(kernel, n_tok, n_head), out_shape=tuple(...  39 us

profile of v8, /device:TPU:24, one launch (start us, length us, event | category | flops | bytes accessed | tf_op | source)
XLA Modules:
  0.0 40.4 jit_solution(8889746648972204637)
XLA Ops:
  0.6 39.0 %shard_map.103 = (bf16[128,1024]{1,0:T(8,128)(2,1)S(1)}, bf16[128,128]{1,0:T(8,128)(2,1)S(1)}, bf16[128,128]{1,0:T(8,128)(2,1)S(1)}) custom-call(bf16[128,1024]{1,0:T(8,128)(2,1)} %query_hbm.1, bf16[16,1024]{1,0:T(8,128)(2,1)} %keys_hbm.1, bf16[16,1024]{1,0:T(8,128)(2,1)} %values_hbm.1, bf16[128,1024]{1,0:T(8,128)(2,1)} %outgrad_hbm.1, f32[8,128]{1,0:T(8,128)} %norm_hbm.1, ...), custom_call_target="tpu_custom_call" | custom-call | tf_op jit(solution)/shard_map/pallas_call | solution.py:506
  39.7 0.8 %shard_map.104 = (bf16[128,1024]{1,0:T(8,128)(2,1)}, bf16[128,128]{1,0:T(8,128)(2,1)}, bf16[128,128]{1,0:T(8,128)(2,1)}) custom-call(bf16[128,1024]{1,0:T(8,128)(2,1)S(1)} %get-tuple-element.6.dq_ref, bf16[128,128]{1,0:T(8,128)(2,1)S(1)} %get-tuple-element.7.dk_ref, bf16[128,128]{1,0:T(8,128)(2,1)S(1)} %get-tuple-element.8.dv_ref), custom_call_target="tpu_custom_call" | custom-call | tf_op jit(solution)/shard_map/pallas_call | solution.py:542
